TPU v7x, 256 devices: a whole 4x4x8 slice. The times are simulated.
256 devices in a mesh: row: 8 (over x, y_lo), col: 32 (over y_hi, z, core).
Axes of the slice: x: 4, y: 4 (y_hi: 2, y_lo: 2; y = y_hi * 2 + y_lo), z: 8, core: 2. Of those that a mesh axis runs over, the one named last changes fastest.
Arguments:
- g_start: float32 [4096, 32768], P('row', 'col'), may hold values from -6 to 6
- cotangent: float32 [4096, 32768], P('row', 'col'), may hold values from -6 to 6
- damping: float32 [32768], replicated, may hold values from 0.1 to 3
- hopping: float32 [6, 32768], replicated, may hold values from -4 to 4
- bonds: int32 [7, 32768], replicated, may hold values 0 or 1
- source: float32 [7, 32768], replicated, may hold values from -5 to 5
Outputs:
- g_end: float32 [4096, 32768], P('row', 'col')
- g_adjoint: float32 [4096, 32768], P('row', 'col')
All inputs are finite; a program needn't handle non-finite values.
Results may differ from a plain program's by a relative error of at most 0.00002.
Values sent between devices are 32-bit elements; how exact they have to be, the bound alone decides.
A program may use at most 128 MiB of HBM per device.

v0:
```python
import jax
import jax.numpy as jnp
from jax import lax
from jax.sharding import PartitionSpec as P

LX = 128


DT = 0.1


def padded(cells, sides, width):
    for axis, dim in sides:
        count = lax.axis_size(axis)
        head = lax.slice_in_dim(cells, 0, width, axis=dim)
        tail = lax.slice_in_dim(cells, cells.shape[dim] - width, cells.shape[dim], axis=dim)
        cells = jnp.concatenate(
            [
                lax.ppermute(tail, axis, [(i, (i + 1) % count) for i in range(count)]),
                cells,
                lax.ppermute(head, axis, [((i + 1) % count, i) for i in range(count)]),
            ],
            axis=dim,
        )
    return cells


def band_offsets(side):
    return (0, 1, -1, 2, -2, 2 * side, -2 * side)


def keep_slab(block, first_row, total_rows):
    glob = first_row + lax.iota(jnp.int32, block.shape[0])
    valid = (glob >= 0) & (glob < total_rows)
    return jnp.where(valid[:, None], block, 0.0)


def joint_faces(block, width, first_row, total_rows):
    extended = padded(block, (("row", 0), ("col", 1)), width)
    extended = keep_slab(extended, first_row - width, total_rows)
    return (extended[:, width:-width], extended[width:-width, :])


def shards(g_start, cotangent, damping, hopping, bonds, source):
    rows_dev, cols_dev = g_start.shape
    modes = damping.shape[0]
    reach = 2 * LX
    offsets = band_offsets(LX)
    total_rows = rows_dev * lax.axis_size("row")
    row_first = lax.axis_index("row") * rows_dev
    col_first = lax.axis_index("col") * cols_dev
    coef = jnp.concatenate([-damping[None, :], hopping], axis=0) * bonds.astype(jnp.float32)
    coef_rows = jnp.pad(coef, ((0, 0), (2 * reach, 2 * reach)))
    coef_cols = jnp.concatenate([coef[:, modes - 2 * reach :], coef, coef[:, : 2 * reach]], axis=1)
    source_rows = jnp.pad(source, ((0, 0), (2 * reach, 2 * reach)))

    def forward_rate(rows_ext, cols_ext, out_row, out_col):
        count_rows = cols_ext.shape[0]
        count_cols = rows_ext.shape[1]
        band_rows = lax.dynamic_slice_in_dim(coef_rows, out_row + 2 * reach, count_rows, 1)
        band_cols = lax.dynamic_slice_in_dim(coef_cols, out_col + 2 * reach, count_cols, 1)
        feed_rows = lax.dynamic_slice_in_dim(source_rows, out_row + 2 * reach, count_rows, 1)
        glob_rows = out_row + lax.iota(jnp.int32, count_rows)
        glob_cols = jnp.mod(out_col + lax.iota(jnp.int32, count_cols), modes)
        rate = jnp.zeros((count_rows, count_cols), jnp.float32)
        for index, offset in enumerate(offsets):
            rate = (
                rate
                + band_rows[index][:, None]
                * rows_ext[reach + offset : reach + offset + count_rows, :]
            )
            rate = (
                rate
                + cols_ext[:, reach + offset : reach + offset + count_cols]
                * band_cols[index][None, :]
            )
            target = jnp.mod(glob_rows + offset, modes)
            rate = rate + jnp.where(
                glob_cols[None, :] == target[:, None], feed_rows[index][:, None], 0.0
            )
        return rate

    def adjoint_rate(rows_ext, cols_ext, out_row, out_col):
        count_rows = cols_ext.shape[0]
        count_cols = rows_ext.shape[1]
        band_rows = lax.dynamic_slice_in_dim(coef_rows, out_row + reach, count_rows + 2 * reach, 1)
        band_cols = lax.dynamic_slice_in_dim(coef_cols, out_col + reach, count_cols + 2 * reach, 1)
        rate = jnp.zeros((count_rows, count_cols), jnp.float32)
        for index, offset in enumerate(offsets):
            weighted_rows = rows_ext * band_rows[index][:, None]
            rate = rate + weighted_rows[reach - offset : reach - offset + count_rows, :]
            weighted_cols = cols_ext * band_cols[index][None, :]
            rate = rate + weighted_cols[:, reach - offset : reach - offset + count_cols]
        return rate

    def extend(block):
        return joint_faces(block, reach, row_first, total_rows)

    def advance(block, rate_fn):
        rows_ext, cols_ext = extend(block)
        first_rate = rate_fn(rows_ext, cols_ext, row_first, col_first)
        middle = block + 0.5 * DT * first_rate
        rows_mid, cols_mid = extend(middle)
        second_rate = rate_fn(rows_mid, cols_mid, row_first, col_first)
        return block + DT * second_rate

    g_end = advance(g_start, forward_rate)
    g_adjoint = advance(cotangent, adjoint_rate)
    return (g_end, g_adjoint)


def solution(mesh):
    return jax.shard_map(
        shards,
        mesh=mesh,
        in_specs=(P("row", "col"), P("row", "col"), P(), P(), P(), P()),
        out_specs=(P("row", "col"), P("row", "col")),
        check_vma=False,
    )
```

profile of v0, /device:TPU:6, one launch (start us, length us, event | category | flops | bytes accessed | tf_op | source)
XLA Modules:
  0.0 294.5 jit_solution(8910241052685975322)
XLA Ops:
  0.6 1.8 fusion.77
  2.5 1.9 collective-permute-start.1
  4.6 0.2 fusion.75
  4.8 2.8 collective-permute-start.9
  7.6 1.0 collective-permute-start.8
  8.7 0.3 maximum_multiply_fusion
  9.0 85.2 %collective-permute-done.8 = f32[256,1024]{1,0:T(8,128)S(1)} collective-permute-done((f32[256,1024]{1,0:T(8,128)S(1)}, f32[256,1024]{1,0:T(8,128)S(1)}, u32[]{:S(2)}, u32[]{:S(2)}) %collective-permute-start.8) | collective-permute-done | bytes 1048608 | tf_op jit(solution)/shard_map/ppermute | solution.py:19
  94.3 0.2 constant_dynamic-update-slice_fusion.4
  94.6 0.3 collective-permute-done.9
  95.0 1.6 fusion.72
  96.6 1.1 copy-done.8
  97.7 7.1 %collective-permute-start.11 = (f32[1024,256]{1,0:T(8,128)}, f32[1024,256]{1,0:T(8,128)}, u32[]{:S(2)}, u32[]{:S(2)}) collective-permute-start(f32[1024,256]{1,0:T(8,128)} %get-tuple-element.12), channel_id=1, source_target_pairs={{1,0},{2,1},{3,2},{4,3},{5,4},{6,5},{7,6},{8,7},{9,8},{10,9},{11,1... | collective-permute-start | bytes 3145736 | tf_op jit(solution)/shard_map/ppermute | solution.py:21
  104.8 0.2 constant_dynamic-update-slice_fusion.1
  105.2 1.6 fusion.73
  106.8 1.0 copy-done.9
  107.8 5.4 %collective-permute-start.3 = (f32[1024,256]{1,0:T(8,128)}, f32[1024,256]{1,0:T(8,128)}, u32[]{:S(2)}, u32[]{:S(2)}) collective-permute-start(f32[1024,256]{1,0:T(8,128)} %get-tuple-element.16), channel_id=1, source_target_pairs={{1,0},{2,1},{3,2},{4,3},{5,4},{6,5},{7,6},{8,7},{9,8},{10,9},{11,1... | collective-permute-start | bytes 3145736 | tf_op jit(solution)/shard_map/ppermute | solution.py:21
  113.5 0.2 pad_dynamic-slice_fusion.12
  113.7 0.6 slice.549
  114.3 0.6 slice.570
  114.9 0.6 slice.566
  115.5 0.7 slice.562
  116.2 0.7 slice.558
  116.8 0.7 slice.554
  117.5 0.6 slice.574
  118.2 0.7 slice.564
  118.8 0.7 slice.560
  119.5 0.7 slice.556
  120.1 0.6 slice.576
  120.8 0.5 add_select_fusion.7
  121.3 0.6 add_select_fusion
  121.9 0.5 add_select_fusion.5
  122.4 0.6 add_select_fusion.3
  123.0 0.6 add_select_fusion.1
  123.7 0.7 pad_dynamic-slice_fusion.18
  124.3 1.7 pad_dynamic-slice_fusion.5
  126.0 2.7 collective-permute-done.2
  128.7 5.4 %maximum_select_fusion.2 = (f32[1024,1536]{1,0:T(8,128)S(1)}, f32[1024,1536]{1,0:T(8,128)S(1)}) fusion(f32[1024,256]{1,0:T(8,128)} %collective-permute-done.11, f32[1024,1024]{1,0:T(8,128)} %copy-done.8, f32[1024,256]{1,0:T(8,128)S(1)} %collective-permute-done.10, pred[1024]{0:T(1024)(128)(4,1)S(1)} %fusion.64, f32[1024,256]{1,0:T(8,128)} %collective-permute-done.3, ...), kind=kLoop, calls=%fused_computation.2 | loop fusion | flops 9437184 | bytes 25166848 | tf_op jit(solution)/shard_map/jit(_where)/select_n | solution.py:35
  134.2 0.2 slice.550
  134.6 0.3 slice.547
  135.0 1.0 copy-done.2
  136.2 6.7 %fusion.25 = f32[512,1024]{1,0:T(8,128)S(1)} fusion(f32[512,1024]{1,0:T(8,128)S(1)} %copy-done.2, f32[1024,1536]{1,0:T(8,128)S(1)} %get-tuple-element.58, f32[512]{0:T(512)S(1)} %bitcast.72, f32[1024]{0:T(1024)S(1)} %bitcast.32, f32[512]{0:T(512)S(1)} %bitcast.58, f32[512]{0:T(512)S(1)} %bitcast.62, f32[1024]{0:T(1024)S(1)} %bitcast.42, f32[512]{0:T(512)S(1)} %bitcast.48, ...), kind=kLoop, calls=%fused_computation.45 | loop fusion | flops 25690112 | bytes 31533056 | tf_op jit(solution)/shard_map/add | solution.py:102
  143.2 1.4 collective-permute-start.4
  144.6 1.8 collective-permute-start.5
  146.5 5.3 %fusion.45 = f32[512,1024]{1,0:T(8,128)S(1)} fusion(f32[512,1024]{1,0:T(8,128)S(1)} %copy-done.5, f32[512,1536]{1,0:T(8,128)S(1)} %slice.550, f32[1024,1024]{1,0:T(8,128)S(1)} %slice.547, f32[1024]{0:T(1024)S(1)} %copy-done.19, f32[512]{0:T(512)S(1)} %copy-done.42, f32[1024]{0:T(1024)S(1)} %slice.572, f32[512]{0:T(512)S(1)} %copy-done.37, ...), kind=kLoop, calls=%fused_computation.80 | loop fusion | flops 15204352 | bytes 33597440 | tf_op jit(solution)/shard_map/add | solution.py:102
  151.8 0.2 fusion.74
  152.0 0.3 collective-permute-start.12
  152.4 2.7 collective-permute-start.13
  155.0 57.5 %collective-permute-done.4 = f32[256,1024]{1,0:T(8,128)S(1)} collective-permute-done((f32[256,1024]{1,0:T(8,128)S(1)}, f32[256,1024]{1,0:T(8,128)S(1)}, u32[]{:S(2)}, u32[]{:S(2)}) %collective-permute-start.4) | collective-permute-done | bytes 1048608 | tf_op jit(solution)/shard_map/ppermute | solution.py:19
  212.8 0.8 copy-done.10
  213.6 5.8 %collective-permute-start.7 = (f32[1024,256]{1,0:T(8,128)S(1)}, f32[1024,256]{1,0:T(8,128)}, u32[]{:S(2)}, u32[]{:S(2)}) collective-permute-start(f32[1024,256]{1,0:T(8,128)S(1)} %get-tuple-element.14), channel_id=1, source_target_pairs={{1,0},{2,1},{3,2},{4,3},{5,4},{6,5},{7,6},{8,7},{9,8},{10,9},{11,1... | collective-permute-start | bytes 3145736 | tf_op jit(solution)/shard_map/ppermute | solution.py:21
  219.3 24.5 %collective-permute-done.12 = f32[256,1024]{1,0:T(8,128)S(1)} collective-permute-done((f32[256,1024]{1,0:T(8,128)S(1)}, f32[256,1024]{1,0:T(8,128)S(1)}, u32[]{:S(2)}, u32[]{:S(2)}) %collective-permute-start.12) | collective-permute-done | bytes 1048608 | tf_op jit(solution)/shard_map/ppermute | solution.py:19
  243.9 1.2 collective-permute-done.13
  245.3 0.8 copy-done.12
  246.1 6.7 %collective-permute-start.15 = (f32[1024,256]{1,0:T(8,128)S(1)}, f32[1024,256]{1,0:T(8,128)}, u32[]{:S(2)}, u32[]{:S(2)}) collective-permute-start(f32[1024,256]{1,0:T(8,128)S(1)} %get-tuple-element.10), channel_id=1, source_target_pairs={{1,0},{2,1},{3,2},{4,3},{5,4},{6,5},{7,6},{8,7},{9,8},{10,9},{11,1... | collective-permute-start | bytes 3145736 | tf_op jit(solution)/shard_map/ppermute | solution.py:21
  252.8 12.6 %collective-permute-done.14 = f32[1024,256]{1,0:T(8,128)} collective-permute-done((f32[1024,256]{1,0:T(8,128)S(1)}, f32[1024,256]{1,0:T(8,128)}, u32[]{:S(2)}, u32[]{:S(2)}) %collective-permute-start.14) | collective-permute-done | bytes 1048608 | tf_op jit(solution)/shard_map/ppermute | solution.py:19
  265.4 9.2 %maximum_select_fusion.3 = (f32[1024,1536]{1,0:T(8,128)}, f32[1024,1536]{1,0:T(8,128)}) fusion(f32[1024,256]{1,0:T(8,128)} %collective-permute-done.15, f32[256,1024]{1,0:T(8,128)} %copy-done.12, f32[512,1024]{1,0:T(8,128)} %copy-done, f32[256,1024]{1,0:T(8,128)} %copy-done.11, f32[1024,256]{1,0:T(8,128)} %collective-permute-done.14, ...), kind=kLoop, calls=%fused_computation.3 | loop fusion | flops 15728640 | bytes 25166848 | tf_op jit(solution)/shard_map/jit(_where)/select_n | solution.py:35
  274.7 2.2 slice.582
  276.9 1.5 copy-done.7
  278.4 0.4 slice.579
  278.8 0.8 slice-done
  279.6 0.8 slice-done.1
  280.4 0.6 copy-done.3
  281.0 7.5 %fusion.27 = f32[512,1024]{1,0:T(8,128)} fusion(f32[512,1024]{1,0:T(8,128)S(1)} %copy-done.3, f32[1024,1536]{1,0:T(8,128)S(1)} %bitcast.30, f32[512]{0:T(512)S(1)} %bitcast.73, f32[1024]{0:T(1024)S(1)} %bitcast.33, f32[512]{0:T(512)S(1)} %bitcast.59, f32[512]{0:T(512)S(1)} %bitcast.63, f32[1024]{0:T(1024)S(1)} %bitcast.43, f32[512]{0:T(512)S(1)} %bitcast.49, ...), kind=kLoop, calls=%fused_computation.47 | loop fusion | flops 25690112 | bytes 31533056 | tf_op jit(solution)/shard_map/add | solution.py:105
  288.6 6.0 %fusion.30 = f32[512,1024]{1,0:T(8,128)} fusion(f32[512,1024]{1,0:T(8,128)S(1)} %copy-done.6, f32[512,1536]{1,0:T(8,128)S(1)} %slice.582, f32[1024,1024]{1,0:T(8,128)S(1)} %slice.579, f32[1024]{0:T(1024)S(1)} %copy-done.19, f32[512]{0:T(512)S(1)} %copy-done.42, f32[1024]{0:T(1024)S(1)} %slice.572, f32[512]{0:T(512)S(1)} %copy-done.37, f32[1024]{0:T(1024)S(1)} %slice.568, ...), kind=kLoop, calls=%fused_computation.51 | loop fusion | flops 15204352 | bytes 33597440 | tf_op jit(solution)/shard_map/add | solution.py:105
  (127 shorter events, 1.7 us)
Async XLA Ops:
  0.6 4.0 %copy-start.4 = (f32[512,1024]{1,0:T(8,128)S(1)}, f32[512,1024]{1,0:T(8,128)}, u32[]{:S(2)}) copy-start(f32[512,1024]{1,0:T(8,128)} %param.7) | copy-start | bytes 6291460
  2.5 102.6 %collective-permute-start.1 = (f32[256,1024]{1,0:T(8,128)S(1)}, f32[256,1024]{1,0:T(8,128)S(1)}, u32[]{:S(2)}, u32[]{:S(2)}) collective-permute-start(f32[256,1024]{1,0:T(8,128)S(1)} %get-tuple-element.23), channel_id=1, source_target_pairs={{32,0},{64,32},{96,64},{128,96},{160,128},{192,160},{224,192},{0,2... | collective-permute-start | bytes 3145736 | tf_op jit(solution)/shard_map/ppermute | solution.py:21
  4.4 4.3 %copy-start.15 = (f32[32768]{0:T(1024)S(1)}, f32[32768]{0:T(1024)}, u32[]{:S(2)}) copy-start(f32[32768]{0:T(1024)} %param.8) | copy-start | bytes 393220
  4.4 4.3 %copy-start.13 = (f32[6,32768]{1,0:T(8,128)S(1)}, f32[6,32768]{1,0:T(8,128)}, u32[]{:S(2)}) copy-start(f32[6,32768]{1,0:T(8,128)} %param.9) | copy-start | bytes 2359300
  4.4 4.3 %copy-start.14 = (s32[7,32768]{1,0:T(8,128)S(1)}, s32[7,32768]{1,0:T(8,128)}, u32[]{:S(2)}) copy-start(s32[7,32768]{1,0:T(8,128)} %param.10) | copy-start | bytes 2752516
  4.4 100.3 %collective-permute-start = (f32[256,1024]{1,0:T(8,128)S(1)}, f32[256,1024]{1,0:T(8,128)S(1)}, u32[]{:S(2)}, u32[]{:S(2)}) collective-permute-start(f32[256,1024]{1,0:T(8,128)S(1)} %get-tuple-element.24), channel_id=1, source_target_pairs={{0,32},{32,64},{64,96},{96,128},{128,160},{160,192},{192,224},{224... | collective-permute-start | bytes 3145736 | tf_op jit(solution)/shard_map/ppermute | solution.py:19
  4.8 90.0 %collective-permute-start.9 = (f32[256,1024]{1,0:T(8,128)S(1)}, f32[256,1024]{1,0:T(8,128)S(1)}, u32[]{:S(2)}, u32[]{:S(2)}) collective-permute-start(f32[256,1024]{1,0:T(8,128)S(1)} %get-tuple-element.19), channel_id=1, source_target_pairs={{32,0},{64,32},{96,64},{128,96},{160,128},{192,160},{224,192},{0,2... | collective-permute-start | bytes 3145736 | tf_op jit(solution)/shard_map/ppermute | solution.py:21
  7.6 86.6 %collective-permute-start.8 = (f32[256,1024]{1,0:T(8,128)S(1)}, f32[256,1024]{1,0:T(8,128)S(1)}, u32[]{:S(2)}, u32[]{:S(2)}) collective-permute-start(f32[256,1024]{1,0:T(8,128)S(1)} %get-tuple-element.20), channel_id=1, source_target_pairs={{0,32},{32,64},{64,96},{96,128},{128,160},{160,192},{192,224},{224... | collective-permute-start | bytes 3145736 | tf_op jit(solution)/shard_map/ppermute | solution.py:19
  95.0 2.7 copy-start.8
  96.6 8.3 %copy-start.1 = (f32[512,1024]{1,0:T(8,128)S(1)}, f32[512,1024]{1,0:T(8,128)}, u32[]{:S(2)}) copy-start(f32[512,1024]{1,0:T(8,128)} %param.6) | copy-start | bytes 6291460
  97.7 28.4 %collective-permute-start.10 = (f32[1024,256]{1,0:T(8,128)}, f32[1024,256]{1,0:T(8,128)S(1)}, u32[]{:S(2)}, u32[]{:S(2)}) collective-permute-start(f32[1024,256]{1,0:T(8,128)} %get-tuple-element.11), channel_id=1, source_target_pairs={{0,1},{1,2},{2,3},{3,4},{4,5},{5,6},{6,7},{7,8},{8,9},{9,10},{10,1... | collective-permute-start | bytes 3145736 | tf_op jit(solution)/shard_map/ppermute | solution.py:19
  97.7 28.4 %collective-permute-start.11 = (f32[1024,256]{1,0:T(8,128)}, f32[1024,256]{1,0:T(8,128)}, u32[]{:S(2)}, u32[]{:S(2)}) collective-permute-start(f32[1024,256]{1,0:T(8,128)} %get-tuple-element.12), channel_id=1, source_target_pairs={{1,0},{2,1},{3,2},{4,3},{5,4},{6,5},{7,6},{8,7},{9,8},{10,9},{11,1... | collective-permute-start | bytes 3145736 | tf_op jit(solution)/shard_map/ppermute | solution.py:21
  105.2 2.6 copy-start.9
  107.8 20.9 %collective-permute-start.2 = (f32[1024,256]{1,0:T(8,128)}, f32[1024,256]{1,0:T(8,128)}, u32[]{:S(2)}, u32[]{:S(2)}) collective-permute-start(f32[1024,256]{1,0:T(8,128)} %get-tuple-element.15), channel_id=1, source_target_pairs={{0,1},{1,2},{2,3},{3,4},{4,5},{5,6},{6,7},{7,8},{8,9},{9,10},{10,1... | collective-permute-start | bytes 3145736 | tf_op jit(solution)/shard_map/ppermute | solution.py:19
  107.8 20.9 %collective-permute-start.3 = (f32[1024,256]{1,0:T(8,128)}, f32[1024,256]{1,0:T(8,128)}, u32[]{:S(2)}, u32[]{:S(2)}) collective-permute-start(f32[1024,256]{1,0:T(8,128)} %get-tuple-element.16), channel_id=1, source_target_pairs={{1,0},{2,1},{3,2},{4,3},{5,4},{6,5},{7,6},{8,7},{9,8},{10,9},{11,1... | collective-permute-start | bytes 3145736 | tf_op jit(solution)/shard_map/ppermute | solution.py:21
  120.8 13.4 %copy-start.49 = (pred[1024]{0:T(1024)(128)(4,1)}, pred[1024]{0:T(1024)(128)(4,1)S(1)}, u32[]{:S(2)}) copy-start(pred[1024]{0:T(1024)(128)(4,1)S(1)} %fusion.64) | copy-start | bytes 3076
  134.4 1.6 copy-start.2
  134.4 1.6 copy-start.20
  134.4 1.6 copy-start.21
  134.4 1.6 copy-start.22
  134.4 1.6 copy-start.23
  134.5 1.6 copy-start.24
  134.5 1.6 copy-start.25
  134.5 1.6 copy-start.26
  134.5 1.6 copy-start.27
  134.5 1.6 copy-start.28
  134.5 1.6 copy-start.29
  134.5 1.6 copy-start.30
  134.5 1.6 copy-start.31
  134.5 1.6 copy-start.32
  134.5 1.6 copy-start.33
  134.6 1.6 copy-start.34
  134.6 1.6 copy-start.35
  134.6 1.6 copy-start.43
  134.6 1.6 copy-start.44
  134.6 1.6 copy-start.45
  134.6 1.6 copy-start.46
  142.9 3.5 %copy-start.5 = (f32[512,1024]{1,0:T(8,128)S(1)}, f32[512,1024]{1,0:T(8,128)}, u32[]{:S(2)}) copy-start(f32[512,1024]{1,0:T(8,128)} %param.7) | copy-start | bytes 6291460
  143.0 3.4 %copy-start.16 = (f32[1024]{0:T(1024)S(1)}, f32[1024]{0:T(1024)}, u32[]{:S(2)}) copy-start(f32[1024]{0:T(1024)} %slice.564) | copy-start | bytes 12292
  143.0 3.4 %copy-start.17 = (f32[1024]{0:T(1024)S(1)}, f32[1024]{0:T(1024)}, u32[]{:S(2)}) copy-start(f32[1024]{0:T(1024)} %slice.560) | copy-start | bytes 12292
  143.0 3.4 %copy-start.18 = (f32[1024]{0:T(1024)S(1)}, f32[1024]{0:T(1024)}, u32[]{:S(2)}) copy-start(f32[1024]{0:T(1024)} %slice.556) | copy-start | bytes 12292
  143.0 3.4 %copy-start.19 = (f32[1024]{0:T(1024)S(1)}, f32[1024]{0:T(1024)}, u32[]{:S(2)}) copy-start(f32[1024]{0:T(1024)} %slice.576) | copy-start | bytes 12292
  143.0 3.4 %copy-start.36 = (f32[512]{0:T(512)S(1)}, f32[512]{0:T(512)}, u32[]{:S(2)}) copy-start(f32[512]{0:T(512)} %slice.549) | copy-start | bytes 6148
  143.0 3.4 %copy-start.37 = (f32[512]{0:T(512)S(1)}, f32[512]{0:T(512)}, u32[]{:S(2)}) copy-start(f32[512]{0:T(512)} %slice.570) | copy-start | bytes 6148
  143.0 3.4 %copy-start.38 = (f32[512]{0:T(512)S(1)}, f32[512]{0:T(512)}, u32[]{:S(2)}) copy-start(f32[512]{0:T(512)} %slice.566) | copy-start | bytes 6148
  143.0 3.4 %copy-start.39 = (f32[512]{0:T(512)S(1)}, f32[512]{0:T(512)}, u32[]{:S(2)}) copy-start(f32[512]{0:T(512)} %slice.562) | copy-start | bytes 6148
  143.0 3.4 %copy-start.40 = (f32[512]{0:T(512)S(1)}, f32[512]{0:T(512)}, u32[]{:S(2)}) copy-start(f32[512]{0:T(512)} %slice.558) | copy-start | bytes 6148
  143.0 3.4 %copy-start.41 = (f32[512]{0:T(512)S(1)}, f32[512]{0:T(512)}, u32[]{:S(2)}) copy-start(f32[512]{0:T(512)} %slice.554) | copy-start | bytes 6148
  143.1 3.4 %copy-start.42 = (f32[512]{0:T(512)S(1)}, f32[512]{0:T(512)}, u32[]{:S(2)}) copy-start(f32[512]{0:T(512)} %slice.574) | copy-start | bytes 6148
  143.2 69.3 %collective-permute-start.4 = (f32[256,1024]{1,0:T(8,128)S(1)}, f32[256,1024]{1,0:T(8,128)S(1)}, u32[]{:S(2)}, u32[]{:S(2)}) collective-permute-start(f32[256,1024]{1,0:T(8,128)S(1)} %get-tuple-element.21), channel_id=1, source_target_pairs={{0,32},{32,64},{64,96},{96,128},{128,160},{160,192},{192,224},{224... | collective-permute-start | bytes 3145736 | tf_op jit(solution)/shard_map/ppermute | solution.py:19
  144.6 67.9 %collective-permute-start.5 = (f32[256,1024]{1,0:T(8,128)S(1)}, f32[256,1024]{1,0:T(8,128)S(1)}, u32[]{:S(2)}, u32[]{:S(2)}) collective-permute-start(f32[256,1024]{1,0:T(8,128)S(1)} %get-tuple-element.22), channel_id=1, source_target_pairs={{32,0},{64,32},{96,64},{128,96},{160,128},{192,160},{224,192},{0,2... | collective-permute-start | bytes 3145736 | tf_op jit(solution)/shard_map/ppermute | solution.py:21
  151.8 93.3 %copy-start = (f32[512,1024]{1,0:T(8,128)}, f32[512,1024]{1,0:T(8,128)S(1)}, u32[]{:S(2)}) copy-start(f32[512,1024]{1,0:T(8,128)S(1)} %fusion.45) | copy-start | bytes 6291460
  152.0 91.9 %collective-permute-start.12 = (f32[256,1024]{1,0:T(8,128)S(1)}, f32[256,1024]{1,0:T(8,128)S(1)}, u32[]{:S(2)}, u32[]{:S(2)}) collective-permute-start(f32[256,1024]{1,0:T(8,128)S(1)} %get-tuple-element.17), channel_id=1, source_target_pairs={{0,32},{32,64},{64,96},{96,128},{128,160},{160,192},{192,224},{224... | collective-permute-start | bytes 3145736 | tf_op jit(solution)/shard_map/ppermute | solution.py:19
  152.4 92.7 %collective-permute-start.13 = (f32[256,1024]{1,0:T(8,128)S(1)}, f32[256,1024]{1,0:T(8,128)S(1)}, u32[]{:S(2)}, u32[]{:S(2)}) collective-permute-start(f32[256,1024]{1,0:T(8,128)S(1)} %get-tuple-element.18), channel_id=1, source_target_pairs={{32,0},{64,32},{96,64},{128,96},{160,128},{192,160},{224,192},{0,2... | collective-permute-start | bytes 3145736 | tf_op jit(solution)/shard_map/ppermute | solution.py:21
  213.6 39.3 %collective-permute-start.6 = (f32[1024,256]{1,0:T(8,128)S(1)}, f32[1024,256]{1,0:T(8,128)}, u32[]{:S(2)}, u32[]{:S(2)}) collective-permute-start(f32[1024,256]{1,0:T(8,128)S(1)} %get-tuple-element.13), channel_id=1, source_target_pairs={{0,1},{1,2},{2,3},{3,4},{4,5},{5,6},{6,7},{7,8},{8,9},{9,10},{10,1... | collective-permute-start | bytes 3145736 | tf_op jit(solution)/shard_map/ppermute | solution.py:19
  213.6 51.8 %copy-start.50 = (pred[1024]{0:T(1024)(128)(4,1)S(1)}, pred[1024]{0:T(1024)(128)(4,1)}, u32[]{:S(2)}) copy-start(pred[1024]{0:T(1024)(128)(4,1)} %copy-done.49) | copy-start | bytes 3076
  213.6 39.3 %collective-permute-start.7 = (f32[1024,256]{1,0:T(8,128)S(1)}, f32[1024,256]{1,0:T(8,128)}, u32[]{:S(2)}, u32[]{:S(2)}) collective-permute-start(f32[1024,256]{1,0:T(8,128)S(1)} %get-tuple-element.14), channel_id=1, source_target_pairs={{1,0},{2,1},{3,2},{4,3},{5,4},{6,5},{7,6},{8,7},{9,8},{10,9},{11,1... | collective-permute-start | bytes 3145736 | tf_op jit(solution)/shard_map/ppermute | solution.py:21
  246.1 19.3 %collective-permute-start.14 = (f32[1024,256]{1,0:T(8,128)S(1)}, f32[1024,256]{1,0:T(8,128)}, u32[]{:S(2)}, u32[]{:S(2)}) collective-permute-start(f32[1024,256]{1,0:T(8,128)S(1)} %get-tuple-element.9), channel_id=1, source_target_pairs={{0,1},{1,2},{2,3},{3,4},{4,5},{5,6},{6,7},{7,8},{8,9},{9,10},{10,1... | collective-permute-start | bytes 3145736 | tf_op jit(solution)/shard_map/ppermute | solution.py:19
  246.1 19.3 %collective-permute-start.15 = (f32[1024,256]{1,0:T(8,128)S(1)}, f32[1024,256]{1,0:T(8,128)}, u32[]{:S(2)}, u32[]{:S(2)}) collective-permute-start(f32[1024,256]{1,0:T(8,128)S(1)} %get-tuple-element.10), channel_id=1, source_target_pairs={{1,0},{2,1},{3,2},{4,3},{5,4},{6,5},{7,6},{8,7},{9,8},{10,9},{11,1... | collective-permute-start | bytes 3145736 | tf_op jit(solution)/shard_map/ppermute | solution.py:21
  274.7 3.7 %copy-start.7 = (f32[1024,1536]{1,0:T(8,128)S(1)}, f32[1024,1536]{1,0:T(8,128)}, u32[]{:S(2)}) copy-start(f32[1024,1536]{1,0:T(8,128)} %get-tuple-element.55) | copy-start | bytes 18874372
  274.7 5.0 %slice-start = ((s8[6291456]{0:T(1024)(128)(4,1)}), s8[4194304]{0:T(1024)(128)(4,1)S(1)}, s32[]{:S(2)}) async-start(s8[6291456]{0:T(1024)(128)(4,1)} %bitcast.29), calls=%async_computation | async-start | bytes 8388608
  278.4 2.1 slice-start.1
  278.4 2.7 copy-start.3
  281.0 7.5 %copy-start.6 = (f32[512,1024]{1,0:T(8,128)S(1)}, f32[512,1024]{1,0:T(8,128)}, u32[]{:S(2)}) copy-start(f32[512,1024]{1,0:T(8,128)} %param.7) | copy-start | bytes 6291460
  (5 other events, 6.5 us)
where the time goes:
time: 295 us
  waiting for transfers between devices  184 us (62%)
  other arithmetic  43.8 us (15%)
  starting transfers between devices  37.1 us (13%)
  local copies, waits for them, and re-layouts  28.1 us (10%)
    ppermute x8, waiting for transfers between devices, padded(): lax.ppermute(tail, axis, [(i, (i + 1) % count) for i in range(count)])  183 us
    ppermute x8, starting transfers between devices, padded(): lax.ppermute(head, axis, [((i + 1) % count, i) for i in range(count)])  34.1 us
    select_n x2, other arithmetic, keep_slab(): return jnp.where(valid[:, None], block, 0.0)  14.7 us
    add x2, other arithmetic, advance(): return block + DT * second_rate  13.5 us
    add x2, other arithmetic, advance(): middle = block + 0.5 * DT * first_rate  12 us
    unnamed x110, local copies, waits for them, and re-layouts  9.25 us
  transfers between devices with their start and end apart: 16, of which 7 were waited for; matrix products, arithmetic and copies ran while one was open for 8% of the time, Pallas kernels for 0%

commit v1 on v0

v1 whole, which is shorter than its diff:
```python
import functools

import jax
import jax.numpy as jnp
from jax import lax
from jax.experimental import pallas as pl
from jax.experimental.pallas import tpu as pltpu
from jax.sharding import PartitionSpec as P

LX = 128
DT = 0.1
MESH = pl.DeviceIdType.MESH
STEPS = 8
AHEAD = 3
CHUNK = 32
LANES = 128


def band_offsets(side):
    return (0, 1, -1, 2, -2, 2 * side, -2 * side)


MIRROR = (0, 2, 1, 4, 3, 6, 5)


def kernel(
    tile,
    n_rows,
    n_cols,
    group,
    g_hbm,
    c_hbm,
    row_tab,
    col_tab,
    g_out,
    c_out,
    ext,
    mid,
    fin,
    row_coef,
    load_sem,
    store_sem,
    send_sem,
    recv_sem,
):
    T = tile
    offsets = band_offsets(T // 2)
    r = lax.axis_index("row")
    c = lax.axis_index("col")
    odd = lax.rem(r, 2)
    even = 1 - odd
    partner = r + 1 - 2 * odd
    other = r - 1 + 2 * odd
    has_b = jnp.logical_and(other >= 0, other < n_rows)
    fwd_row = r + 2 - 4 * odd
    has_fwd = jnp.logical_and(fwd_row >= 0, fwd_row < n_rows)
    src_row = r - 2 + 4 * odd
    left = lax.rem(c + n_cols - 1, n_cols)
    right = lax.rem(c + 1, n_cols)
    left_edge = lax.rem(c, group) == 0
    right_edge = lax.rem(c, group) == group - 1
    sides = ((left, left_edge), (right, right_edge))

    a_heavy = odd * T + even * 4 * T
    a_light = even * 5 * T
    b_heavy = odd * 4 * T + even * T
    b_light = odd * 5 * T
    a_mid = a_heavy - T
    b_mid = b_heavy - T
    own_a = 2 * T + even * T
    own_b = 2 * T + odd * T

    def aligned(value, step=None):
        return pl.multiple_of(value, T if step is None else step)

    def box(f, row, col, rows=T, cols=T):
        return ext.at[f, pl.ds(aligned(row), rows), pl.ds(aligned(col), cols)]

    def remote(src, dst, f, index, to):
        return pltpu.make_async_remote_copy(
            src_ref=src,
            dst_ref=dst,
            send_sem=send_sem.at[f, index],
            recv_sem=recv_sem.at[f, index],
            device_id=to,
            device_id_type=MESH,
        )

    def order(s):
        return lax.rem(3 * (s // 2), 4), lax.rem(s, 2)

    def rung_copy(f, s):
        q, heavy = order(s)
        half = odd * (1 - heavy) + even * heavy
        there = odd * (5 * T - heavy * T) + even * heavy * T
        return remote(
            box(f, 2 * T + half * T, 2 * T + q * T),
            box(f, there, 2 * T + q * T),
            f,
            s,
            (partner, c),
        )

    def arrived_row(heavy):
        return odd * heavy * T + even * (5 * T - heavy * T)

    def rail_copy(f, s):
        q, heavy = order(s)
        there = odd * (4 * T + heavy * T) + even * (T - heavy * T)
        return remote(
            box(f, arrived_row(heavy), 2 * T + q * T),
            box(f, there, 2 * T + q * T),
            f,
            STEPS + s,
            (fwd_row, c),
        )

    def side_index(side, message):
        return 2 * STEPS + 6 * side + message

    def there_col(side, far):
        return (6 * T + far * T) if side == 0 else (T - far * T)

    def here_col(side, far):
        return (2 * T + far * T) if side == 0 else (5 * T - far * T)

    def tile_copy(f, side, far, half, row, to):
        return remote(
            box(f, row, here_col(side, far)),
            box(f, 2 * T + half * T, there_col(side, far)),
            f,
            side_index(side, 2 * far + half),
            to,
        )

    def corner_copy(f, side, down, row, to):
        return remote(
            box(f, row, here_col(side, 0)),
            box(f, T + 3 * T * down, there_col(side, 0)),
            f,
            side_index(side, 4 + down),
            to,
        )

    def own_columns(f):
        for side, (col, edge) in enumerate(sides):
            @pl.when(jnp.logical_not(edge))
            def _():
                for far in range(2):
                    for half in range(2):
                        tile_copy(f, side, far, half, 2 * T + half * T, (r, col)).start()

            @pl.when(edge)
            def _():
                corner_copy(f, side, odd, 2 * T + even * T, (partner, col)).start()

                @pl.when(has_b)
                def _():
                    corner_copy(f, side, even, 2 * T + odd * T, (other, col)).start()

    def pass_tile(f, s):
        k = s // 2
        q = (3 * k) % 4
        heavy = s % 2
        side = 0 if q < 2 else 1
        far = 1 if q in (1, 2) else 0
        col, edge = sides[side]

        @pl.when(edge)
        def _():
            half = odd * heavy + even * (1 - heavy)
            tile_copy(f, side, far, half, arrived_row(heavy), (partner, col)).start()

    def pass_corners(f, side):
        col, edge = sides[side]

        @pl.when(jnp.logical_not(edge))
        def _():
            corner_copy(f, side, even, a_heavy, (r, col)).start()

            @pl.when(has_b)
            def _():
                corner_copy(f, side, odd, b_heavy, (r, col)).start()

    def wait_tile(f, side, far):
        for half in range(2):
            tile_copy(f, 1 - side, far, half, 2 * T, (r, c)).wait_recv()

    def wait_corners(f, side):
        corner_copy(f, 1 - side, even, 2 * T, (r, c)).wait_recv()

        @pl.when(has_b)
        def _():
            corner_copy(f, 1 - side, odd, 2 * T, (r, c)).wait_recv()

    def rate(f, src, row, col, coef_row, col_bands):
        wide = src[pl.ds(row, CHUNK), pl.ds(col - LANES, T + 2 * LANES)]
        tall = src[pl.ds(row - 8, CHUNK + 16), pl.ds(col, T)]

        def rows_of(k):
            band = row_coef[f, k, pl.ds(coef_row, CHUNK), :]
            return jnp.concatenate([band] * (T // LANES), axis=1)

        total = tall[8 : 8 + CHUNK] * (rows_of(0) + col_bands[0])
        for k, offset in enumerate(offsets):
            if k == 0:
                continue
            if abs(offset) < 8:
                by_row = pltpu.roll(tall, (-offset) % (CHUNK + 16), 0)[8 : 8 + CHUNK]
                by_col = pltpu.roll(wide, (-offset) % (T + 2 * LANES), 1)[:, LANES : LANES + T]
            else:
                by_row = src[pl.ds(row + offset, CHUNK), pl.ds(col, T)]
                by_col = src[pl.ds(row, CHUNK), pl.ds(col + offset, T)]
            total = total + rows_of(k) * by_row + col_bands[k] * by_col
        return total

    def bands_at(f, b):
        block = col_tab[pl.ds(aligned(f * 8, 8), 8), pl.ds(aligned((b + 1) * T), T)]
        return [jnp.broadcast_to(block[k : k + 1], (CHUNK, T)) for k in range(7)]

    def add_source(f, dst, row, col, coef_row, b, scale):
        tiles = n_cols * 4
        shift = lax.rem(4 * c + b - 2 * r - (coef_row // T - 1) + 2 * tiles + 1, tiles)

        @pl.when(jnp.logical_and(f == 0, shift <= 2))
        def _():
            def body(i, carry):
                values = row_tab[pl.ds(pl.multiple_of(coef_row + i * 8, 8), 8), :]
                here = lax.broadcasted_iota(jnp.int32, (8, T), 1) - lax.broadcasted_iota(
                    jnp.int32, (8, T), 0
                )
                here = here + (shift - 1) * T - i * 8
                at = pl.ds(pl.multiple_of(row + i * 8, 8), 8)
                total = dst[at, pl.ds(col, T)]
                for k, offset in enumerate(offsets):
                    feed = jnp.broadcast_to(values[:, 14 + k : 15 + k], (8, T))
                    total = total + jnp.where(here == offset, scale * feed, 0.0)
                dst[at, pl.ds(col, T)] = total
                return carry

            lax.fori_loop(0, T // 8, body, 0)

    def mid_tile(f, row, b):
        row = aligned(row)
        col = (b + 2) * T
        col_bands = bands_at(f, b)
        field = ext.at[f]

        def body(i, carry):
            at = pl.multiple_of(row + i * CHUNK, CHUNK)
            total = rate(f, field, at, col, pl.multiple_of(at - T, CHUNK), col_bands)
            total = total + field[pl.ds(at, CHUNK), pl.ds(col, T)]
            mid[pl.ds(pl.multiple_of(at - T, CHUNK), CHUNK), pl.ds(col - T, T)] = total
            return carry

        lax.fori_loop(0, T // CHUNK, body, 0)
        add_source(f, mid, aligned(row - T), col - T, aligned(row - T), b, 1.0)

    def own_mid(f, b):
        mid_tile(f, 2 * T, b)
        mid_tile(f, 3 * T, b)

    def mid_a(f, b):
        mid_tile(f, a_heavy, b)

    def mid_b(f, b):
        @pl.when(has_b)
        def _():
            mid_tile(f, b_heavy, b)

    def store_copy(k, half, b):
        out = (g_out, c_out)[k]
        rows, cols = pl.ds(aligned(half * T), T), pl.ds(b * T, T)
        return pltpu.make_async_copy(fin.at[k, rows, cols], out.at[rows, cols], store_sem.at[k, half * 4 + b])

    def out_tile(f, half, b):
        col_bands = bands_at(f, b)
        col = (b + 1) * T
        field = ext.at[f]
        done = fin.at[f]
        base = aligned(half * T)

        def body(i, carry):
            at = pl.multiple_of(base + i * CHUNK, CHUNK)
            inner = pl.multiple_of(at + T, CHUNK)
            total = rate(f, mid, inner, col, inner, col_bands)
            total = field[pl.ds(pl.multiple_of(at + 2 * T, CHUNK), CHUNK), pl.ds(col + T, T)] + 2.0 * total
            done[pl.ds(at, CHUNK), pl.ds(b * T, T)] = total
            return carry

        lax.fori_loop(0, T // CHUNK, body, 0)
        add_source(f, done, base, b * T, aligned(base + T), b, 2.0)
        for k in range(2):
            @pl.when(f == k)
            def _():
                store_copy(k, half, b).start()

    def out_pair(f, b):
        out_tile(f, 0, b)
        out_tile(f, 1, b)

    half_a = even
    half_b = odd

    def finish(f):
        wait_tile(f, 1, 1)
        own_mid(f, 4)
        out_pair(f, 3)

        @pl.when(has_b)
        def _():
            rail_copy(f, STEPS - 1).wait_recv()

        mid_b(f, 1)
        out_tile(f, half_b, 1)

    def tasks(f, s):
        if s == 1:
            pass_corners(f, 0)
        if s == 3:
            pass_corners(f, 1)
            wait_tile(f, 1, 0)
            own_mid(f, 3)
        if s == 5:
            wait_corners(f, 1)
            wait_tile(f, 0, 0)
            own_mid(f, 0)
            own_mid(f, 2)
            mid_a(f, 3)
            mid_b(f, 3)
        if s == 7:
            wait_corners(f, 0)
            wait_tile(f, 0, 1)
            own_mid(f, 1)
            own_mid(f, -1)
            for b in (0, 1, 2):
                mid_a(f, b)
            for b in (0, 2):
                mid_b(f, b)
            out_pair(f, 0)
            out_pair(f, 2)
            out_tile(f, half_a, 1)

    loads = [
        pltpu.make_async_copy(src, ext.at[k, pl.ds(2 * T, 2 * T), pl.ds(2 * T, 4 * T)], load_sem.at[k])
        for k, src in enumerate((g_hbm, c_hbm))
    ]
    for load in loads:
        load.start()

    barrier = pltpu.get_barrier_semaphore()

    def greet(row, col):
        pl.semaphore_signal(barrier, inc=1, device_id=(row, col), device_id_type=MESH)

    greet(partner, c)
    both = has_b.astype(jnp.int32)
    pl.when(has_fwd)(lambda: greet(fwd_row, c))
    pl.when(has_b)(lambda: greet(src_row, c))
    for col, edge in sides:
        pl.when(jnp.logical_not(edge))(lambda: greet(r, col))
        pl.when(edge)(lambda: greet(partner, col))
        pl.when(jnp.logical_and(edge, has_b))(lambda: greet(other, col))
    edges = left_edge.astype(jnp.int32) + right_edge.astype(jnp.int32)
    peers = 3 + has_fwd.astype(jnp.int32) + both + edges * both

    @pl.when(jnp.logical_not(has_b))
    def _():
        for k in range(2):
            ext[k, pl.ds(aligned(b_heavy), T), pl.ds(T, 6 * T)] = jnp.zeros((T, 6 * T), jnp.float32)
        mid[pl.ds(aligned(b_mid), T), :] = jnp.zeros((T, 6 * T), jnp.float32)

    pl.semaphore_wait(barrier, peers)
    loads[0].wait()
    for s in range(AHEAD):
        rung_copy(0, s).start()
    own_columns(0)
    loads[1].wait()

    def spread(i, carry):
        at = pl.ds(pl.multiple_of(i * 8, 8), 8)
        values = row_tab[at, :]
        for k in range(14):
            row_coef[k // 7, k % 7, at, :] = jnp.broadcast_to(values[:, k : k + 1], (8, LANES))
        return carry

    lax.fori_loop(0, 4 * T // 8, spread, 0)

    def field_steps(f, carry):
        for s in range(STEPS):
            rung_copy(f, s).wait_recv()
            pl.when(has_fwd)(lambda: rail_copy(f, s).start())
            pass_tile(f, s)
            if s + AHEAD < STEPS:
                rung_copy(f, s + AHEAD).start()
            else:
                pl.when(f == 0)(lambda: rung_copy(1, s + AHEAD - STEPS).start())
            if s == 4:
                pl.when(f == 0)(lambda: own_columns(1))
            if s == 0:
                pl.when(f == 1)(lambda: finish(0))
            else:
                pl.when(has_b)(lambda: rail_copy(f, s - 1).wait_recv())
            tasks(f, s)
        return carry

    lax.fori_loop(0, 2, field_steps, 0)
    finish(1)

    def drain(f, carry):
        for s in range(STEPS):
            rung_copy(f, s).wait_send()
            pl.when(has_fwd)(lambda: rail_copy(f, s).wait_send())
        for side in range(2):
            for far in range(2):
                for half in range(2):
                    tile_copy(f, side, far, half, 2 * T, (r, c)).wait_send()
            _, edge = sides[side]
            first = even + edge.astype(jnp.int32) * (odd - even)
            corner_copy(f, side, first, 2 * T, (r, c)).wait_send()
            second = 1 - first
            pl.when(has_b)(lambda: corner_copy(f, side, second, 2 * T, (r, c)).wait_send())
        return carry

    lax.fori_loop(0, 2, drain, 0)
    for half in range(2):
        for b in range(4):
            for k in range(2):
                store_copy(k, half, b).wait()


def shards(tile, n_rows, n_cols, group, g_start, cotangent, damping, hopping, bonds, source):
    T = tile
    modes = damping.shape[0]
    rows_dev, cols_dev = g_start.shape
    offsets = band_offsets(T // 2)
    row_first = lax.axis_index("row") * rows_dev
    col_first = lax.axis_index("col") * cols_dev
    coef = jnp.concatenate([-damping[None, :], hopping], axis=0) * bonds.astype(jnp.float32)
    both = (0.5 * DT) * jnp.concatenate([coef, source], axis=0)
    wrapped = jnp.concatenate([both[:, modes - 2 * T :], both, both[:, : 6 * T]], axis=1)
    near_rows = lax.dynamic_slice_in_dim(wrapped, row_first, 6 * T, 1)
    near_cols = lax.dynamic_slice_in_dim(wrapped, col_first, 8 * T, 1)

    def pick(window, count):
        forward = window[:7, T : T + count]
        adjoint = jnp.stack(
            [window[MIRROR[k], T + o : T + o + count] for k, o in enumerate(offsets)]
        )
        return forward, adjoint

    row_f, row_a = pick(near_rows, 4 * T)
    col_f, col_a = pick(near_cols, 6 * T)
    row_tab = jnp.concatenate([row_f, row_a, near_rows[7:, T : 5 * T]], axis=0)
    row_tab = jnp.pad(row_tab, ((0, LANES - 21), (0, 0))).T
    blank = jnp.zeros((1, 6 * T), jnp.float32)
    col_tab = jnp.concatenate([col_f, blank, col_a, blank], axis=0)

    block = jax.ShapeDtypeStruct((rows_dev, cols_dev), jnp.float32)
    sems = 2 * STEPS + 12
    return pl.pallas_call(
        functools.partial(kernel, T, n_rows, n_cols, group),
        out_shape=(block, block),
        in_specs=[
            pl.BlockSpec(memory_space=pl.ANY),
            pl.BlockSpec(memory_space=pl.ANY),
            pl.BlockSpec(memory_space=pltpu.VMEM),
            pl.BlockSpec(memory_space=pltpu.VMEM),
        ],
        out_specs=(pl.BlockSpec(memory_space=pl.ANY), pl.BlockSpec(memory_space=pl.ANY)),
        scratch_shapes=[
            pltpu.VMEM((2, 6 * T, 8 * T), jnp.float32),
            pltpu.VMEM((4 * T, 6 * T), jnp.float32),
            pltpu.VMEM((2, 2 * T, 4 * T), jnp.float32),
            pltpu.VMEM((2, 7, 4 * T, LANES), jnp.float32),
            pltpu.SemaphoreType.DMA((2,)),
            pltpu.SemaphoreType.DMA((2, 8)),
            pltpu.SemaphoreType.DMA((2, sems)),
            pltpu.SemaphoreType.DMA((2, sems)),
        ],
        compiler_params=pltpu.CompilerParams(
            collective_id=0, has_side_effects=True, vmem_limit_bytes=56 * 2**20
        ),
    )(g_start, cotangent, row_tab, col_tab)


def build(mesh, tile):
    n_rows = mesh.shape["row"]
    n_cols = mesh.shape["col"]
    return jax.shard_map(
        functools.partial(shards, tile, n_rows, n_cols, n_cols // 2),
        mesh=mesh,
        in_specs=(P("row", "col"), P("row", "col"), P(), P(), P(), P()),
        out_specs=(P("row", "col"), P("row", "col")),
        check_vma=False,
    )


def solution(mesh):
    return build(mesh, 2 * LX)
```

time: 295 us -> 172 us (0.58)
  waiting for transfers between devices: 184 us -> 0 us
  Pallas kernels: 0 us -> 160 us
  other arithmetic: 43.8 us -> 3.39 us
  starting transfers between devices: 37.1 us -> 0 us
  local copies, waits for them, and re-layouts: 28.1 us -> 7.65 us
    ppermute x16 -> x0, waiting for transfers between devices: 184 us -> none  [the longest x8 183 us: padded(): lax.ppermute(tail, axis, [(i, (i + 1) % count) for i in range(count)])]
    pallas_call x0 -> x1, Pallas kernels: none -> 160 us  [shards(): pl.pallas_call(functools.partial(kernel, T, n_rows, n_cols, group), out_s...]
    ppermute x16 -> x0, starting transfers between devices: 37.1 us -> none  [the longest x8 34.1 us: padded(): lax.ppermute(head, axis, [((i + 1) % count, i) for i in range(count)])]
    add x4 -> x0, other arithmetic: 25.5 us -> none  [the longest x2 13.5 us: advance(): return block + DT * second_rate]
    slice x29 -> x6, local copies, waits for them, and re-layouts: 18.6 us -> 0.46 us  [the longest x2 0.34 us: pick(): window[MIRROR[k], T + o:T + o + count]]
    select_n x7 -> x0, other arithmetic: 17.6 us -> none  [the longest x2 14.7 us: keep_slab(): return jnp.where(valid[:, None], block, 0.0)]
    unnamed x110 -> x6, local copies, waits for them, and re-layouts: 9.25 us -> 4.63 us
  transfers between devices with their start and end apart: 16 -> 0, of which waited for: 7 -> 0; matrix products, arithmetic and copies ran while one was open for 8% -> 0% of each run, Pallas kernels for 0% -> 0%
where the time goes in v1:
time: 172 us; the launch traced here: 171 us
  Pallas kernels  160 us (93%)
  local copies, waits for them, and re-layouts  7.65 us (4%)
  other arithmetic  3.39 us (2%)
    pallas_call x1, Pallas kernels, shards(): pl.pallas_call(functools.partial(kernel, T, n_rows, n_cols, group), out_s...  160 us
    unnamed x6, local copies, waits for them, and re-layouts  4.63 us

profile of v1, /device:TPU:6, one launch (start us, length us, event | category | flops | bytes accessed | tf_op | source)
XLA Modules:
  0.0 171.4 jit_solution(5220105181265736025)
XLA Ops:
  0.6 0.0 copy-start.1
  0.6 1.0 neg.6
  1.7 1.8 %maximum_multiply_fusion.1 = f32[7,32768]{1,0:T(8,128)S(1)} fusion(f32[6,32768]{1,0:T(8,128)} %param.9, f32[1,32768]{1,0:T(1,128)S(1)} %bitcast.3, s32[7,32768]{1,0:T(8,128)} %param.10), kind=kLoop, calls=%fused_computation.2 | loop fusion | flops 688128 | bytes 2752512 | tf_op jit(solution)/shard_map/mul | solution.py:439
  3.5 0.0 copy-done.1
  3.5 0.4 maximum_multiply_fusion
  3.9 0.1 pad_maximum_fusion
  4.1 0.2 fusion.2
  4.3 0.2 fusion
  4.5 0.1 fusion.1
  4.6 1.3 concatenate.19.col_tab
  5.9 0.2 concatenate.18
  6.1 1.0 copy.8.row_tab
  7.1 159.6 %shard_map.77 = (f32[512,1024]{1,0:T(8,128)}, f32[512,1024]{1,0:T(8,128)}) custom-call(f32[512,1024]{1,0:T(8,128)} %g_hbm.1, f32[512,1024]{1,0:T(8,128)} %c_hbm.1, f32[1024,128]{1,0:T(8,128)} %copy.8.row_tab, f32[16,1536]{1,0:T(8,128)} %concatenate.19.col_tab), custom_call_target="tpu_custom_call" | custom-call | tf_op jit(solution)/shard_map/pallas_call | solution.py:461
  166.8 0.0 copy-start
  166.8 3.3 %copy.11 = f32[512,1024]{1,0:T(8,128)} copy(f32[512,1024]{1,0:T(8,128)} %get-tuple-element.20) | data formatting | bytes 4194304
  170.1 0.0 copy-done
  170.1 1.3 copy.12
  (5 shorter events, 0.1 us)
Async XLA Ops:
  0.6 2.9 %copy-start.1 = (f32[7,32768]{1,0:T(8,128)S(1)}, f32[7,32768]{1,0:T(8,128)}, u32[]{:S(2)}) copy-start(f32[7,32768]{1,0:T(8,128)} %param.11) | copy-start | bytes 2752516
  166.8 3.3 %copy-start = (f32[512,1024]{1,0:T(8,128)S(1)}, f32[512,1024]{1,0:T(8,128)}, u32[]{:S(2)}) copy-start(f32[512,1024]{1,0:T(8,128)} %get-tuple-element.21) | copy-start | bytes 6291460

commit v2 on v1

v2 whole, which is shorter than its diff:
```python
import functools

import jax
import jax.numpy as jnp
from jax import lax
from jax.experimental import pallas as pl
from jax.experimental.pallas import tpu as pltpu
from jax.sharding import PartitionSpec as P

LX = 128
DT = 0.1
MESH = pl.DeviceIdType.MESH
STEPS = 8
AHEAD = 3
CHUNK = 32
LANES = 128


def band_offsets(side):
    return (0, 1, -1, 2, -2, 2 * side, -2 * side)


MIRROR = (0, 2, 1, 4, 3, 6, 5)


def kernel(
    tile,
    n_rows,
    n_cols,
    group,
    g_hbm,
    c_hbm,
    damping,
    hopping,
    bonds,
    source,
    g_out,
    c_out,
    ext,
    mid,
    fin,
    row_coef,
    col_tab,
    row_tab,
    win_damping,
    win_hopping,
    win_bonds,
    win_source,
    win_coef,
    load_sem,
    win_sem,
    store_sem,
    send_sem,
    recv_sem,
):
    T = tile
    offsets = band_offsets(T // 2)
    modes = 4 * T * n_cols
    r = lax.axis_index("row")
    c = lax.axis_index("col")
    odd = lax.rem(r, 2)
    even = 1 - odd
    partner = r + 1 - 2 * odd
    other = r - 1 + 2 * odd
    has_b = jnp.logical_and(other >= 0, other < n_rows)
    fwd_row = r + 2 - 4 * odd
    has_fwd = jnp.logical_and(fwd_row >= 0, fwd_row < n_rows)
    src_row = r - 2 + 4 * odd
    left = lax.rem(c + n_cols - 1, n_cols)
    right = lax.rem(c + 1, n_cols)
    left_edge = lax.rem(c, group) == 0
    right_edge = lax.rem(c, group) == group - 1
    sides = ((left, left_edge), (right, right_edge))

    def row_at(p):
        return T * (odd * (4 - p) + even * (1 + p))

    a_heavy = row_at(3)
    b_heavy = row_at(0)
    half_a = even
    half_b = odd

    def aligned(value, step=None):
        return pl.multiple_of(value, T if step is None else step)

    def box(f, row, col, rows=T, cols=T):
        return ext.at[f, pl.ds(aligned(row), rows), pl.ds(aligned(col), cols)]

    def remote(src, dst, f, index, to):
        return pltpu.make_async_remote_copy(
            src_ref=src,
            dst_ref=dst,
            send_sem=send_sem.at[f, index],
            recv_sem=recv_sem.at[f, index],
            device_id=to,
            device_id_type=MESH,
        )

    def order(s):
        return lax.rem(3 * lax.rem(s, 4), 4), s // 4

    def rung_copy(f, s):
        q, heavy = order(s)
        half = odd * (1 - heavy) + even * heavy
        there = odd * (5 * T - heavy * T) + even * heavy * T
        return remote(
            box(f, 2 * T + half * T, 2 * T + q * T),
            box(f, there, 2 * T + q * T),
            f,
            s,
            (partner, c),
        )

    def arrived_row(heavy):
        return odd * heavy * T + even * (5 * T - heavy * T)

    def rail_copy(f, s):
        q, heavy = order(s)
        there = odd * (4 * T + heavy * T) + even * (T - heavy * T)
        return remote(
            box(f, arrived_row(heavy), 2 * T + q * T),
            box(f, there, 2 * T + q * T),
            f,
            STEPS + s,
            (fwd_row, c),
        )

    def side_index(side, message):
        return 2 * STEPS + 6 * side + message

    def there_col(side, far):
        return (6 * T + far * T) if side == 0 else (T - far * T)

    def here_col(side, far):
        return (2 * T + far * T) if side == 0 else (5 * T - far * T)

    def tile_copy(f, side, far, half, row, to):
        return remote(
            box(f, row, here_col(side, far)),
            box(f, 2 * T + half * T, there_col(side, far)),
            f,
            side_index(side, 2 * far + half),
            to,
        )

    def corner_copy(f, side, down, row, to):
        return remote(
            box(f, row, here_col(side, 0)),
            box(f, T + 3 * T * down, there_col(side, 0)),
            f,
            side_index(side, 4 + down),
            to,
        )

    def own_columns(f):
        for side, (col, edge) in enumerate(sides):
            @pl.when(jnp.logical_not(edge))
            def _():
                for far in range(2):
                    for half in range(2):
                        tile_copy(f, side, far, half, 2 * T + half * T, (r, col)).start()

            @pl.when(edge)
            def _():
                corner_copy(f, side, odd, 2 * T + even * T, (partner, col)).start()

                @pl.when(has_b)
                def _():
                    corner_copy(f, side, even, 2 * T + odd * T, (other, col)).start()

    def pass_tile(f, s):
        q = (3 * (s % 4)) % 4
        heavy = s // 4
        side = 0 if q < 2 else 1
        far = 1 if q in (1, 2) else 0
        col, edge = sides[side]

        @pl.when(edge)
        def _():
            half = odd * heavy + even * (1 - heavy)
            tile_copy(f, side, far, half, arrived_row(heavy), (partner, col)).start()

    def pass_a_corner(f, side):
        col, edge = sides[side]

        @pl.when(jnp.logical_not(edge))
        def _():
            corner_copy(f, side, even, a_heavy, (r, col)).start()

    def pass_b_corner(f, side):
        col, edge = sides[side]

        @pl.when(jnp.logical_and(has_b, jnp.logical_not(edge)))
        def _():
            corner_copy(f, side, odd, b_heavy, (r, col)).start()

    def wait_tile(f, side, far, half):
        tile_copy(f, 1 - side, far, half, 2 * T, (r, c)).wait_recv()

    def wait_a_corner(f, side):
        corner_copy(f, 1 - side, even, 2 * T, (r, c)).wait_recv()

    def wait_b_corner(f, side):
        @pl.when(has_b)
        def _():
            corner_copy(f, 1 - side, odd, 2 * T, (r, c)).wait_recv()

    def spread_lanes(band):
        return jnp.concatenate([band] * (T // LANES), axis=1)

    def rate(f, src, row, col, coef_row, col_bands):
        wide = src[pl.ds(row, CHUNK), pl.ds(aligned(col - LANES, LANES), T + 2 * LANES)]
        tall = src[pl.ds(aligned(row - 8, 8), CHUNK + 16), pl.ds(col, T)]

        def rows_of(k):
            return spread_lanes(row_coef[7 * f + k, pl.ds(coef_row, CHUNK), :])

        total = tall[8 : 8 + CHUNK] * (rows_of(0) + col_bands[0])
        for k, offset in enumerate(offsets):
            if k == 0:
                continue
            if abs(offset) < 8:
                by_row = pltpu.roll(tall, (-offset) % (CHUNK + 16), 0)[8 : 8 + CHUNK]
                by_col = pltpu.roll(wide, (-offset) % (T + 2 * LANES), 1)[:, LANES : LANES + T]
            else:
                by_row = src[pl.ds(aligned(row + offset, CHUNK), CHUNK), pl.ds(col, T)]
                by_col = src[pl.ds(row, CHUNK), pl.ds(aligned(col + offset), T)]
            total = total + rows_of(k) * by_row + col_bands[k] * by_col
        return total

    def bands_at(f, b):
        block = col_tab[pl.ds(aligned(f * 8, 8), 8), pl.ds(aligned((b + 1) * T), T)]
        return [jnp.broadcast_to(block[k : k + 1], (CHUNK, T)) for k in range(7)]

    def add_source(f, dst, row, col, coef_row, b, scale):
        tiles = n_cols * 4
        shift = lax.rem(4 * c + b - 2 * r - (coef_row // T - 1) + 2 * tiles + 1, tiles)

        @pl.when(jnp.logical_and(f == 0, shift <= 2))
        def _():
            def body(i, carry):
                here = lax.broadcasted_iota(jnp.int32, (CHUNK, T), 1) - lax.broadcasted_iota(
                    jnp.int32, (CHUNK, T), 0
                )
                here = here + (shift - 1) * T - i * CHUNK
                at = pl.ds(aligned(row + i * CHUNK, CHUNK), CHUNK)
                total = dst[at, pl.ds(col, T)]
                for k, offset in enumerate(offsets):
                    feed = row_coef[14 + k, pl.ds(aligned(coef_row + i * CHUNK, CHUNK), CHUNK), :]
                    total = total + jnp.where(here == offset, spread_lanes(scale * feed), 0.0)
                dst[at, pl.ds(col, T)] = total
                return carry

            lax.fori_loop(0, T // CHUNK, body, 0)

    def mid_tile(f, row, b):
        row = aligned(row)
        col = aligned((b + 2) * T)
        inner = aligned((b + 1) * T)
        col_bands = bands_at(f, b)
        field = ext.at[f]

        def body(i, carry):
            at = aligned(row + i * CHUNK, CHUNK)
            low = aligned(row - T + i * CHUNK, CHUNK)
            total = rate(f, field, at, col, low, col_bands)
            total = total + field[pl.ds(at, CHUNK), pl.ds(col, T)]
            mid[pl.ds(low, CHUNK), pl.ds(inner, T)] = total
            return carry

        lax.fori_loop(0, T // CHUNK, body, 0, unroll=True)
        add_source(f, mid, aligned(row - T), inner, aligned(row - T), b, 1.0)

    def mids(f, jobs):
        packed = sum((8 * p + b + 1) << (5 * i) for i, (p, b) in enumerate(jobs))

        def body(_, rest):
            p = lax.rem(rest, 32) // 8
            b = lax.rem(rest, 8) - 1

            @pl.when(jnp.logical_or(p > 0, has_b))
            def _():
                mid_tile(f, row_at(p), b)

            return rest // 32

        lax.fori_loop(0, len(jobs), body, jnp.int32(packed))

    def store_copy(k, half, b):
        out = (g_out, c_out)[k]
        rows, cols = pl.ds(aligned(half * T), T), pl.ds(aligned(b * T), T)
        return pltpu.make_async_copy(fin.at[k, rows, cols], out.at[rows, cols], store_sem.at[k, half * 4 + b])

    def out_tile(f, half, b):
        col_bands = bands_at(f, b)
        col = aligned((b + 1) * T)
        outer = aligned((b + 2) * T)
        own = aligned(b * T)
        field = ext.at[f]
        done = fin.at[f]
        base = aligned(half * T)

        def body(i, carry):
            at = aligned(base + i * CHUNK, CHUNK)
            inner = aligned(base + T + i * CHUNK, CHUNK)
            total = rate(f, mid, inner, col, inner, col_bands)
            total = field[pl.ds(aligned(base + 2 * T + i * CHUNK, CHUNK), CHUNK), pl.ds(outer, T)] + 2.0 * total
            done[pl.ds(at, CHUNK), pl.ds(own, T)] = total
            return carry

        lax.fori_loop(0, T // CHUNK, body, 0, unroll=True)
        add_source(f, done, base, own, aligned(base + T), b, 2.0)
        for k in range(2):
            @pl.when(f == k)
            def _():
                store_copy(k, half, b).start()

    def outs(f, jobs):
        packed = sum((4 * e + b) << (3 * i) for i, (e, b) in enumerate(jobs))

        def body(_, rest):
            e = lax.rem(rest, 8) // 4
            b = lax.rem(rest, 4)
            out_tile(f, (1 - e) * half_a + e * half_b, b)
            return rest // 8

        lax.fori_loop(0, len(jobs), body, jnp.int32(packed))

    def finish(f):
        wait_tile(f, 1, 1, half_a)

        @pl.when(has_b)
        def _():
            rail_copy(f, STEPS - 1).wait_recv()

        mids(f, ((2, 4), (0, 1)))
        outs(f, ((0, 3), (1, 1)))

    def tasks(f, s):
        if s == 1:
            pass_b_corner(f, 0)
        if s == 2:
            pass_b_corner(f, 1)
            wait_tile(f, 0, 0, half_b)
            wait_tile(f, 1, 0, half_b)
            mids(f, ((1, 0), (1, 3)))
        if s == 4:
            pass_a_corner(f, 0)
            mids(f, ((1, 2), (1, 1)))
        if s == 5:
            pass_a_corner(f, 1)
            wait_b_corner(f, 0)
            wait_b_corner(f, 1)
            wait_tile(f, 1, 0, half_a)
            wait_tile(f, 1, 1, half_b)
            mids(f, ((0, 0), (2, 3), (1, 4)))
        if s == 6:
            wait_tile(f, 0, 0, half_a)
            wait_tile(f, 0, 1, half_b)
            wait_a_corner(f, 1)
            mids(f, ((1, -1), (2, 0), (2, 2), (0, 3), (3, 3)))
            outs(f, ((1, 0), (1, 3)))
        if s == 7:
            wait_a_corner(f, 0)
            wait_tile(f, 0, 1, half_a)
            mids(f, ((2, 1), (2, -1), (3, 0), (3, 1), (3, 2), (0, 2)))
            outs(f, ((0, 0), (0, 1), (0, 2), (1, 2)))

    row_first = r * 2 * T
    col_first = c * 4 * T
    spans = (
        (0, row_first + modes - 2 * T, 2 * T),
        (2 * T, row_first, 4 * T),
        (6 * T, col_first + modes - 2 * T, 2 * T),
        (8 * T, col_first, 4 * T),
        (12 * T, col_first + 4 * T, 2 * T),
    )
    arrays = (
        (damping, win_damping),
        (hopping, win_hopping),
        (bonds, win_bonds),
        (source, win_source),
    )

    def window_copies():
        for k, (src, dst) in enumerate(arrays):
            for i, (at, first, count) in enumerate(spans):
                start = aligned(lax.rem(first, modes), 2 * T)
                yield pltpu.make_async_copy(
                    src.at[:, pl.ds(start, count)], dst.at[:, pl.ds(at, count)], win_sem.at[k, i]
                )

    loads = [
        pltpu.make_async_copy(src, ext.at[k, pl.ds(2 * T, 2 * T), pl.ds(2 * T, 4 * T)], load_sem.at[k])
        for k, src in enumerate((g_hbm, c_hbm))
    ]
    barrier = pltpu.get_barrier_semaphore()

    def greet(row, col):
        pl.semaphore_signal(barrier, inc=1, device_id=(row, col), device_id_type=MESH)

    greet(partner, c)
    both = has_b.astype(jnp.int32)
    pl.when(has_fwd)(lambda: greet(fwd_row, c))
    pl.when(has_b)(lambda: greet(src_row, c))
    for col, edge in sides:
        pl.when(jnp.logical_not(edge))(lambda: greet(r, col))
        pl.when(edge)(lambda: greet(partner, col))
        pl.when(jnp.logical_and(edge, has_b))(lambda: greet(other, col))
    edges = left_edge.astype(jnp.int32) + right_edge.astype(jnp.int32)
    peers = 3 + has_fwd.astype(jnp.int32) + both + edges * both

    for load in loads:
        load.start()
    for copy in window_copies():
        copy.start()

    loads[0].wait()
    pl.semaphore_wait(barrier, peers)
    for s in range(AHEAD):
        rung_copy(0, s).start()
    own_columns(0)

    @pl.when(jnp.logical_not(has_b))
    def _():
        for k in range(2):
            ext[k, pl.ds(aligned(b_heavy), T), pl.ds(T, 6 * T)] = jnp.zeros((T, 6 * T), jnp.float32)
        mid[pl.ds(aligned(b_heavy - T), T), :] = jnp.zeros((T, 6 * T), jnp.float32)

    for copy in window_copies():
        copy.wait()
    half_step = 0.5 * DT
    present = win_bonds[...].astype(jnp.float32)
    win_coef[0:1, :] = -half_step * win_damping[...] * present[0:1]
    win_coef[1:7, :] = half_step * win_hopping[...] * present[1:7]
    win_coef[7:8, :] = jnp.zeros((1, 14 * T), jnp.float32)

    def adjoint(first, count):
        window = win_coef[:, first : first + count + 2 * T]
        rows = []
        for k, offset in enumerate(offsets):
            band = window[MIRROR[k] : MIRROR[k] + 1]
            rows.append(pltpu.roll(band, (-offset) % (count + 2 * T), 1)[:, T : T + count])
        return rows

    row_tab[...] = jnp.zeros_like(row_tab)
    row_tab[0:8, :] = win_coef[:, T : 5 * T]
    for k, band in enumerate(adjoint(0, 4 * T)):
        row_tab[7 + k : 8 + k, :] = band
    row_tab[14:21, :] = half_step * win_source[:, T : 5 * T]
    col_tab[0:8, :] = win_coef[:, 7 * T : 13 * T]
    for k, band in enumerate(adjoint(6 * T, 6 * T)):
        col_tab[8 + k : 9 + k, :] = band
    for i in range(4 * T // LANES):
        block = row_tab[:, i * LANES : (i + 1) * LANES].T
        for k in range(21):
            row_coef[k, i * LANES : (i + 1) * LANES, :] = jnp.broadcast_to(block[:, k : k + 1], (LANES, LANES))

    loads[1].wait()

    def field_steps(f, carry):
        for s in range(STEPS):
            rung_copy(f, s).wait_recv()
            pl.when(has_fwd)(lambda: rail_copy(f, s).start())
            pass_tile(f, s)
            if s + AHEAD < STEPS:
                rung_copy(f, s + AHEAD).start()
            else:
                pl.when(f == 0)(lambda: rung_copy(1, s + AHEAD - STEPS).start())
            if s == 3:
                pl.when(f == 0)(lambda: own_columns(1))
            if s == 0:
                pl.when(f == 1)(lambda: finish(0))
            else:
                pl.when(has_b)(lambda: rail_copy(f, s - 1).wait_recv())
            tasks(f, s)
        return carry

    lax.fori_loop(0, 2, field_steps, 0)
    finish(1)

    def drain(f, carry):
        for s in range(STEPS):
            rung_copy(f, s).wait_send()
            pl.when(has_fwd)(lambda: rail_copy(f, s).wait_send())
        for side in range(2):
            for far in range(2):
                for half in range(2):
                    tile_copy(f, side, far, half, 2 * T, (r, c)).wait_send()
            _, edge = sides[side]
            first = even + edge.astype(jnp.int32) * (odd - even)
            corner_copy(f, side, first, 2 * T, (r, c)).wait_send()
            pl.when(has_b)(lambda: corner_copy(f, side, 1 - first, 2 * T, (r, c)).wait_send())
        return carry

    lax.fori_loop(0, 2, drain, 0)
    for half in range(2):
        for b in range(4):
            for k in range(2):
                store_copy(k, half, b).wait()


def shards(tile, n_rows, n_cols, group, g_start, cotangent, damping, hopping, bonds, source):
    T = tile
    block = jax.ShapeDtypeStruct(g_start.shape, jnp.float32)
    sems = 2 * STEPS + 12
    anywhere = pl.BlockSpec(memory_space=pl.ANY)
    return pl.pallas_call(
        functools.partial(kernel, T, n_rows, n_cols, group),
        out_shape=(block, block),
        in_specs=[anywhere] * 6,
        out_specs=(anywhere, anywhere),
        scratch_shapes=[
            pltpu.VMEM((2, 6 * T, 8 * T), jnp.float32),
            pltpu.VMEM((4 * T, 6 * T), jnp.float32),
            pltpu.VMEM((2, 2 * T, 4 * T), jnp.float32),
            pltpu.VMEM((21, 4 * T, LANES), jnp.float32),
            pltpu.VMEM((16, 6 * T), jnp.float32),
            pltpu.VMEM((LANES, 4 * T), jnp.float32),
            pltpu.VMEM((1, 14 * T), jnp.float32),
            pltpu.VMEM((6, 14 * T), jnp.float32),
            pltpu.VMEM((7, 14 * T), jnp.int32),
            pltpu.VMEM((7, 14 * T), jnp.float32),
            pltpu.VMEM((8, 14 * T), jnp.float32),
            pltpu.SemaphoreType.DMA((2,)),
            pltpu.SemaphoreType.DMA((4, 5)),
            pltpu.SemaphoreType.DMA((2, 8)),
            pltpu.SemaphoreType.DMA((2, sems)),
            pltpu.SemaphoreType.DMA((2, sems)),
        ],
        compiler_params=pltpu.CompilerParams(
            collective_id=0, has_side_effects=True, vmem_limit_bytes=56 * 2**20
        ),
    )(g_start, cotangent, damping.reshape(1, -1), hopping, bonds, source)


def build(mesh, tile):
    n_rows = mesh.shape["row"]
    n_cols = mesh.shape["col"]
    return jax.shard_map(
        functools.partial(shards, tile, n_rows, n_cols, n_cols // 2),
        mesh=mesh,
        in_specs=(P("row", "col"), P("row", "col"), P(), P(), P(), P()),
        out_specs=(P("row", "col"), P("row", "col")),
        check_vma=False,
    )


def solution(mesh):
    return build(mesh, 2 * LX)
```

time: 172 us -> 120 us (0.70)
  Pallas kernels: 160 us -> 114 us
  other arithmetic: 3.39 us -> 0 us
  local copies, waits for them, and re-layouts: 7.65 us -> 4.63 us
    pallas_call x1, Pallas kernels: 160 us -> 114 us  [shards(): pl.pallas_call(functools.partial(kernel, T, n_rows, n_cols, group), out_s...]
    mul x2 -> x0, other arithmetic: 2.24 us -> none  [the longest x1 1.83 us: shards(): jnp.concatenate([-damping[None, :], hopping], axis=0)]
    unnamed x6 -> x4, local copies, waits for them, and re-layouts: 4.63 us -> 4.63 us
where the time goes in v2:
time: 120 us; the launch traced here: 119 us
  Pallas kernels  114 us (95%)
  local copies, waits for them, and re-layouts  4.63 us (4%)
    pallas_call x1, Pallas kernels, shards(): pl.pallas_call(functools.partial(kernel, T, n_rows, n_cols, group), out_s...  114 us
    unnamed x4, local copies, waits for them, and re-layouts  4.63 us

profile of v2, /device:TPU:6, one launch (start us, length us, event | category | flops | bytes accessed | tf_op | source)
XLA Modules:
  0.0 118.9 jit_solution(17245197682739788258)
XLA Ops:
  0.6 113.6 %shard_map.77 = (f32[512,1024]{1,0:T(8,128)}, f32[512,1024]{1,0:T(8,128)}) custom-call(f32[512,1024]{1,0:T(8,128)} %g_hbm.1, f32[512,1024]{1,0:T(8,128)} %c_hbm.1, f32[1,32768]{1,0:T(1,128)} %bitcast.1, f32[6,32768]{1,0:T(8,128)} %hopping.1, s32[7,32768]{1,0:T(8,128)} %bonds.1, f32[7,32768]{1,0:T(8,128)} %source.1), custom_call_target="tpu_custom_call" | custom-call | tf_op jit(solution)/shard_map/pallas_call | solution.py:508
  114.2 0.0 copy-start
  114.2 3.3 %copy.10 = f32[512,1024]{1,0:T(8,128)} copy(f32[512,1024]{1,0:T(8,128)} %get-tuple-element.4) | data formatting | bytes 4194304
  117.5 0.0 copy-done
  117.6 1.3 %copy.11 = f32[512,1024]{1,0:T(8,128)} copy(f32[512,1024]{1,0:T(8,128)S(1)} %copy-done) | data formatting | bytes 4194304
Async XLA Ops:
  114.2 3.3 %copy-start = (f32[512,1024]{1,0:T(8,128)S(1)}, f32[512,1024]{1,0:T(8,128)}, u32[]{:S(2)}) copy-start(f32[512,1024]{1,0:T(8,128)} %get-tuple-element.5) | copy-start | bytes 6291460

commit v3 on v2

--- a/solution.py
+++ b/solution.py
@@ -12,6 +12,8 @@
 MESH = pl.DeviceIdType.MESH
 STEPS = 8
 AHEAD = 3
+PIECES = (1, 1, 1, 1, 1, 1, 2, 4)
+EXTRA = sum(PIECES) - STEPS
 CHUNK = 32
 LANES = 128
 
@@ -34,11 +36,9 @@
     hopping,
     bonds,
     source,
-    g_out,
-    c_out,
+    fin,
     ext,
     mid,
-    fin,
     row_coef,
     col_tab,
     row_tab,
@@ -49,7 +49,6 @@
     win_coef,
     load_sem,
     win_sem,
-    store_sem,
     send_sem,
     recv_sem,
 ):
@@ -83,8 +82,8 @@
     def aligned(value, step=None):
         return pl.multiple_of(value, T if step is None else step)
 
-    def box(f, row, col, rows=T, cols=T):
-        return ext.at[f, pl.ds(aligned(row), rows), pl.ds(aligned(col), cols)]
+    def box(f, row, col, rows=T):
+        return ext.at[f, pl.ds(aligned(row, rows), rows), pl.ds(aligned(col), T)]
 
     def remote(src, dst, f, index, to):
         return pltpu.make_async_remote_copy(
@@ -97,36 +96,46 @@
         )
 
     def order(s):
-        return lax.rem(3 * lax.rem(s, 4), 4), s // 4
-
-    def rung_copy(f, s):
+        return (3 * (s % 4)) % 4, s // 4
+
+    def piece_of(s, i):
+        rows = T // PIECES[s]
+        return rows, i * rows, sum(PIECES[:s]) + i
+
+    def rung_copy(f, s, i, src=None):
         q, heavy = order(s)
+        rows, first, index = piece_of(s, i)
         half = odd * (1 - heavy) + even * heavy
         there = odd * (5 * T - heavy * T) + even * heavy * T
-        return remote(
-            box(f, 2 * T + half * T, 2 * T + q * T),
-            box(f, there, 2 * T + q * T),
-            f,
-            s,
-            (partner, c),
-        )
+        if src is None:
+            src = box(f, 2 * T + half * T + first, 2 * T + q * T, rows)
+        else:
+            src = src.at[pl.ds(aligned(half * T + first, rows), rows), pl.ds(q * T, T)]
+        return remote(src, box(f, there + first, 2 * T + q * T, rows), f, index, (partner, c))
 
     def arrived_row(heavy):
         return odd * heavy * T + even * (5 * T - heavy * T)
 
-    def rail_copy(f, s):
+    def rail_copy(f, s, i):
         q, heavy = order(s)
+        rows, first, index = piece_of(s, i)
         there = odd * (4 * T + heavy * T) + even * (T - heavy * T)
         return remote(
-            box(f, arrived_row(heavy), 2 * T + q * T),
-            box(f, there, 2 * T + q * T),
+            box(f, arrived_row(heavy) + first, 2 * T + q * T, rows),
+            box(f, there + first, 2 * T + q * T, rows),
             f,
-            STEPS + s,
+            STEPS + EXTRA + index,
             (fwd_row, c),
         )
 
+    def wait_rail(f, s):
+        @pl.when(has_b)
+        def _():
+            for i in range(PIECES[s]):
+                rail_copy(f, s, i).wait_recv()
+
     def side_index(side, message):
-        return 2 * STEPS + 6 * side + message
+        return 2 * (STEPS + EXTRA) + 6 * side + message
 
     def there_col(side, far):
         return (6 * T + far * T) if side == 0 else (T - far * T)
@@ -134,10 +143,10 @@
     def here_col(side, far):
         return (2 * T + far * T) if side == 0 else (5 * T - far * T)
 
-    def tile_copy(f, side, far, half, row, to):
+    def tile_copy(f, side, far, half, row, to, rows=T, first=0):
         return remote(
-            box(f, row, here_col(side, far)),
-            box(f, 2 * T + half * T, there_col(side, far)),
+            box(f, row + first, here_col(side, far), rows),
+            box(f, 2 * T + half * T + first, there_col(side, far), rows),
             f,
             side_index(side, 2 * far + half),
             to,
@@ -168,7 +177,8 @@
                 def _():
                     corner_copy(f, side, even, 2 * T + odd * T, (other, col)).start()
 
-    def pass_tile(f, s):
+    def pass_tile(f, s, i):
+        rows, first, _ = piece_of(s, i)
         q = (3 * (s % 4)) % 4
         heavy = s // 4
         side = 0 if q < 2 else 1
@@ -178,7 +188,7 @@
         @pl.when(edge)
         def _():
             half = odd * heavy + even * (1 - heavy)
-            tile_copy(f, side, far, half, arrived_row(heavy), (partner, col)).start()
+            tile_copy(f, side, far, half, arrived_row(heavy), (partner, col), rows, first).start()
 
     def pass_a_corner(f, side):
         col, edge = sides[side]
@@ -286,11 +296,6 @@
 
         lax.fori_loop(0, len(jobs), body, jnp.int32(packed))
 
-    def store_copy(k, half, b):
-        out = (g_out, c_out)[k]
-        rows, cols = pl.ds(aligned(half * T), T), pl.ds(aligned(b * T), T)
-        return pltpu.make_async_copy(fin.at[k, rows, cols], out.at[rows, cols], store_sem.at[k, half * 4 + b])
-
     def out_tile(f, half, b):
         col_bands = bands_at(f, b)
         col = aligned((b + 1) * T)
@@ -310,10 +315,6 @@
 
         lax.fori_loop(0, T // CHUNK, body, 0, unroll=True)
         add_source(f, done, base, own, aligned(base + T), b, 2.0)
-        for k in range(2):
-            @pl.when(f == k)
-            def _():
-                store_copy(k, half, b).start()
 
     def outs(f, jobs):
         packed = sum((4 * e + b) << (3 * i) for i, (e, b) in enumerate(jobs))
@@ -328,27 +329,28 @@
 
     def finish(f):
         wait_tile(f, 1, 1, half_a)
-
-        @pl.when(has_b)
-        def _():
-            rail_copy(f, STEPS - 1).wait_recv()
-
+        wait_rail(f, 7)
         mids(f, ((2, 4), (0, 1)))
-        outs(f, ((0, 3), (1, 1)))
+        outs(f, ((1, 1), (0, 3)))
 
     def tasks(f, s):
         if s == 1:
+            wait_rail(f, 0)
             pass_b_corner(f, 0)
         if s == 2:
+            wait_rail(f, 1)
             pass_b_corner(f, 1)
             wait_tile(f, 0, 0, half_b)
             wait_tile(f, 1, 0, half_b)
             mids(f, ((1, 0), (1, 3)))
         if s == 4:
             pass_a_corner(f, 0)
+            wait_rail(f, 2)
+            wait_rail(f, 3)
             mids(f, ((1, 2), (1, 1)))
         if s == 5:
             pass_a_corner(f, 1)
+            wait_rail(f, 4)
             wait_b_corner(f, 0)
             wait_b_corner(f, 1)
             wait_tile(f, 1, 0, half_a)
@@ -358,13 +360,18 @@
             wait_tile(f, 0, 0, half_a)
             wait_tile(f, 0, 1, half_b)
             wait_a_corner(f, 1)
+            wait_rail(f, 5)
             mids(f, ((1, -1), (2, 0), (2, 2), (0, 3), (3, 3)))
             outs(f, ((1, 0), (1, 3)))
+            wait_rail(f, 6)
+            mids(f, ((0, 2),))
         if s == 7:
             wait_a_corner(f, 0)
+            mids(f, ((2, 1), (3, 0), (3, 1), (3, 2)))
+            outs(f, ((0, 1), (0, 2), (1, 2)))
             wait_tile(f, 0, 1, half_a)
-            mids(f, ((2, 1), (2, -1), (3, 0), (3, 1), (3, 2), (0, 2)))
-            outs(f, ((0, 0), (0, 1), (0, 2), (1, 2)))
+            mids(f, ((2, -1),))
+            outs(f, ((0, 0),))
 
     row_first = r * 2 * T
     col_first = c * 4 * T
@@ -415,10 +422,10 @@
     for copy in window_copies():
         copy.start()
 
-    loads[0].wait()
     pl.semaphore_wait(barrier, peers)
     for s in range(AHEAD):
-        rung_copy(0, s).start()
+        rung_copy(0, s, 0, g_hbm).start()
+    loads[0].wait()
     own_columns(0)
 
     @pl.when(jnp.logical_not(has_b))
@@ -458,21 +465,24 @@
 
     loads[1].wait()
 
+    def send_block(f, s):
+        for i in range(PIECES[s]):
+            rung_copy(f, s, i).start()
+
     def field_steps(f, carry):
         for s in range(STEPS):
-            rung_copy(f, s).wait_recv()
-            pl.when(has_fwd)(lambda: rail_copy(f, s).start())
-            pass_tile(f, s)
+            for i in range(PIECES[s]):
+                rung_copy(f, s, i).wait_recv()
+                pl.when(has_fwd)(lambda: rail_copy(f, s, i).start())
+                pass_tile(f, s, i)
             if s + AHEAD < STEPS:
-                rung_copy(f, s + AHEAD).start()
+                send_block(f, s + AHEAD)
             else:
-                pl.when(f == 0)(lambda: rung_copy(1, s + AHEAD - STEPS).start())
+                pl.when(f == 0)(lambda: send_block(1, s + AHEAD - STEPS))
             if s == 3:
                 pl.when(f == 0)(lambda: own_columns(1))
             if s == 0:
                 pl.when(f == 1)(lambda: finish(0))
-            else:
-                pl.when(has_b)(lambda: rail_copy(f, s - 1).wait_recv())
             tasks(f, s)
         return carry
 
@@ -481,8 +491,9 @@
 
     def drain(f, carry):
         for s in range(STEPS):
-            rung_copy(f, s).wait_send()
-            pl.when(has_fwd)(lambda: rail_copy(f, s).wait_send())
+            for i in range(PIECES[s]):
+                rung_copy(f, s, i).wait_send()
+                pl.when(has_fwd)(lambda: rail_copy(f, s, i).wait_send())
         for side in range(2):
             for far in range(2):
                 for half in range(2):
@@ -494,26 +505,29 @@
         return carry
 
     lax.fori_loop(0, 2, drain, 0)
-    for half in range(2):
-        for b in range(4):
-            for k in range(2):
-                store_copy(k, half, b).wait()
+
+
+def store_kernel(fin, g_out, c_out, sem):
+    copies = [pltpu.make_async_copy(fin.at[k], out, sem.at[k]) for k, out in enumerate((g_out, c_out))]
+    for copy in copies:
+        copy.start()
+    for copy in copies:
+        copy.wait()
 
 
 def shards(tile, n_rows, n_cols, group, g_start, cotangent, damping, hopping, bonds, source):
     T = tile
     block = jax.ShapeDtypeStruct(g_start.shape, jnp.float32)
-    sems = 2 * STEPS + 12
+    sems = 2 * (STEPS + EXTRA) + 12
     anywhere = pl.BlockSpec(memory_space=pl.ANY)
-    return pl.pallas_call(
+    fin = pl.pallas_call(
         functools.partial(kernel, T, n_rows, n_cols, group),
-        out_shape=(block, block),
+        out_shape=pltpu.VMEM((2,) + g_start.shape, jnp.float32),
         in_specs=[anywhere] * 6,
-        out_specs=(anywhere, anywhere),
+        out_specs=pl.BlockSpec(memory_space=pltpu.VMEM),
         scratch_shapes=[
             pltpu.VMEM((2, 6 * T, 8 * T), jnp.float32),
             pltpu.VMEM((4 * T, 6 * T), jnp.float32),
-            pltpu.VMEM((2, 2 * T, 4 * T), jnp.float32),
             pltpu.VMEM((21, 4 * T, LANES), jnp.float32),
             pltpu.VMEM((16, 6 * T), jnp.float32),
             pltpu.VMEM((LANES, 4 * T), jnp.float32),
@@ -524,14 +538,21 @@
             pltpu.VMEM((8, 14 * T), jnp.float32),
             pltpu.SemaphoreType.DMA((2,)),
             pltpu.SemaphoreType.DMA((4, 5)),
-            pltpu.SemaphoreType.DMA((2, 8)),
             pltpu.SemaphoreType.DMA((2, sems)),
             pltpu.SemaphoreType.DMA((2, sems)),
         ],
         compiler_params=pltpu.CompilerParams(
-            collective_id=0, has_side_effects=True, vmem_limit_bytes=56 * 2**20
+            collective_id=0, has_side_effects=True, vmem_limit_bytes=55 * 2**20
         ),
     )(g_start, cotangent, damping.reshape(1, -1), hopping, bonds, source)
+    return pl.pallas_call(
+        store_kernel,
+        out_shape=(block, block),
+        in_specs=[pl.BlockSpec(memory_space=pltpu.VMEM)],
+        out_specs=(anywhere, anywhere),
+        scratch_shapes=[pltpu.SemaphoreType.DMA((2,))],
+        compiler_params=pltpu.CompilerParams(vmem_limit_bytes=2**20),
+    )(fin)
 
 
 def build(mesh, tile):

time: 120 us -> 116 us (0.967)
  local copies, waits for them, and re-layouts: 4.63 us -> 0 us
    unnamed x4 -> x0, local copies, waits for them, and re-layouts: 4.63 us -> none
    pallas_call x0 -> x1, Pallas kernels: none -> 2.03 us  [shards(): pl.pallas_call(store_kernel, out_shape=(block, block), in_specs=[pl.Block...]
where the time goes in v3:
time: 116 us; the launch traced here: 115 us
  Pallas kernels  115 us (99%)
    pallas_call x1, Pallas kernels, shards(): pl.pallas_call(functools.partial(kernel, T, n_rows, n_cols, group), out_s...  113 us

profile of v3, /device:TPU:6, one launch (start us, length us, event | category | flops | bytes accessed | tf_op | source)
XLA Modules:
  0.0 115.2 jit_solution(11978129150500127047)
XLA Ops:
  0.6 112.5 %shard_map.77.fin = f32[2,512,1024]{2,1,0:T(8,128)S(1)} custom-call(f32[512,1024]{1,0:T(8,128)} %g_hbm.1, f32[512,1024]{1,0:T(8,128)} %c_hbm.1, f32[1,32768]{1,0:T(1,128)} %bitcast.1, f32[6,32768]{1,0:T(8,128)} %hopping.1, s32[7,32768]{1,0:T(8,128)} %bonds.1, f32[7,32768]{1,0:T(8,128)} %source.1), custom_call_target="tpu_custom_call" | custom-call | tf_op jit(solution)/shard_map/pallas_call | solution.py:523
  113.2 2.0 %shard_map.78 = (f32[512,1024]{1,0:T(8,128)}, f32[512,1024]{1,0:T(8,128)}) custom-call(f32[2,512,1024]{2,1,0:T(8,128)S(1)} %shard_map.77.fin), custom_call_target="tpu_custom_call" | custom-call | tf_op jit(solution)/shard_map/pallas_call | solution.py:548

commit v4 on v3

--- a/solution.py
+++ b/solution.py
@@ -12,7 +12,7 @@
 MESH = pl.DeviceIdType.MESH
 STEPS = 8
 AHEAD = 3
-PIECES = (1, 1, 1, 1, 1, 1, 2, 4)
+PIECES = (4, 2, 2, 2, 2, 2, 2, 4)
 EXTRA = sum(PIECES) - STEPS
 CHUNK = 32
 LANES = 128
@@ -269,17 +269,18 @@
         inner = aligned((b + 1) * T)
         col_bands = bands_at(f, b)
         field = ext.at[f]
+        target = mid.at[f]
 
         def body(i, carry):
             at = aligned(row + i * CHUNK, CHUNK)
             low = aligned(row - T + i * CHUNK, CHUNK)
             total = rate(f, field, at, col, low, col_bands)
             total = total + field[pl.ds(at, CHUNK), pl.ds(col, T)]
-            mid[pl.ds(low, CHUNK), pl.ds(inner, T)] = total
+            target[pl.ds(low, CHUNK), pl.ds(inner, T)] = total
             return carry
 
         lax.fori_loop(0, T // CHUNK, body, 0, unroll=True)
-        add_source(f, mid, aligned(row - T), inner, aligned(row - T), b, 1.0)
+        add_source(f, target, aligned(row - T), inner, aligned(row - T), b, 1.0)
 
     def mids(f, jobs):
         packed = sum((8 * p + b + 1) << (5 * i) for i, (p, b) in enumerate(jobs))
@@ -308,7 +309,7 @@
         def body(i, carry):
             at = aligned(base + i * CHUNK, CHUNK)
             inner = aligned(base + T + i * CHUNK, CHUNK)
-            total = rate(f, mid, inner, col, inner, col_bands)
+            total = rate(f, mid.at[f], inner, col, inner, col_bands)
             total = field[pl.ds(aligned(base + 2 * T + i * CHUNK, CHUNK), CHUNK), pl.ds(outer, T)] + 2.0 * total
             done[pl.ds(at, CHUNK), pl.ds(own, T)] = total
             return carry
@@ -327,28 +328,23 @@
 
         lax.fori_loop(0, len(jobs), body, jnp.int32(packed))
 
-    def finish(f):
-        wait_tile(f, 1, 1, half_a)
-        wait_rail(f, 7)
-        mids(f, ((2, 4), (0, 1)))
-        outs(f, ((1, 1), (0, 3)))
-
-    def tasks(f, s):
-        if s == 1:
+    def early(f, s, i):
+        last = i == PIECES[s] - 1
+        if s == 1 and last:
             wait_rail(f, 0)
             pass_b_corner(f, 0)
-        if s == 2:
+        if s == 2 and last:
             wait_rail(f, 1)
             pass_b_corner(f, 1)
             wait_tile(f, 0, 0, half_b)
             wait_tile(f, 1, 0, half_b)
             mids(f, ((1, 0), (1, 3)))
-        if s == 4:
+        if s == 4 and last:
             pass_a_corner(f, 0)
             wait_rail(f, 2)
             wait_rail(f, 3)
             mids(f, ((1, 2), (1, 1)))
-        if s == 5:
+        if s == 5 and last:
             pass_a_corner(f, 1)
             wait_rail(f, 4)
             wait_b_corner(f, 0)
@@ -356,22 +352,38 @@
             wait_tile(f, 1, 0, half_a)
             wait_tile(f, 1, 1, half_b)
             mids(f, ((0, 0), (2, 3), (1, 4)))
-        if s == 6:
+        if s == 6 and last:
             wait_tile(f, 0, 0, half_a)
             wait_tile(f, 0, 1, half_b)
+            mids(f, ((1, -1), (2, 0)))
+        if s == 7 and i == 0:
+            wait_rail(f, 5)
+            mids(f, ((2, 2), (0, 3)))
+        if s == 7 and i == 1:
             wait_a_corner(f, 1)
-            wait_rail(f, 5)
-            mids(f, ((1, -1), (2, 0), (2, 2), (0, 3), (3, 3)))
+            mids(f, ((3, 3),))
+        if s == 7 and i == 2:
             outs(f, ((1, 0), (1, 3)))
+
+    def late(f, part):
+        if part == 0:
+            wait_a_corner(f, 0)
+            mids(f, ((2, 1), (3, 0), (3, 1), (3, 2)))
+        if part == 1:
             wait_rail(f, 6)
             mids(f, ((0, 2),))
-        if s == 7:
-            wait_a_corner(f, 0)
-            mids(f, ((2, 1), (3, 0), (3, 1), (3, 2)))
             outs(f, ((0, 1), (0, 2), (1, 2)))
+        if part == 2:
             wait_tile(f, 0, 1, half_a)
-            mids(f, ((2, -1),))
-            outs(f, ((0, 0),))
+            wait_tile(f, 1, 1, half_a)
+            mids(f, ((2, -1), (2, 4)))
+            outs(f, ((0, 0), (0, 3)))
+        if part == 3:
+            wait_rail(f, 7)
+            mids(f, ((0, 1),))
+            outs(f, ((1, 1),))
+
+    late_at = {(1, 0): 0, (1, 1): 1, (2, 0): 2, (3, 0): 3}
 
     row_first = r * 2 * T
     col_first = c * 4 * T
@@ -424,7 +436,8 @@
 
     pl.semaphore_wait(barrier, peers)
     for s in range(AHEAD):
-        rung_copy(0, s, 0, g_hbm).start()
+        for i in range(PIECES[s]):
+            rung_copy(0, s, i, g_hbm).start()
     loads[0].wait()
     own_columns(0)
 
@@ -432,7 +445,7 @@
     def _():
         for k in range(2):
             ext[k, pl.ds(aligned(b_heavy), T), pl.ds(T, 6 * T)] = jnp.zeros((T, 6 * T), jnp.float32)
-        mid[pl.ds(aligned(b_heavy - T), T), :] = jnp.zeros((T, 6 * T), jnp.float32)
+            mid[k, pl.ds(aligned(b_heavy - T), T), :] = jnp.zeros((T, 6 * T), jnp.float32)
 
     for copy in window_copies():
         copy.wait()
@@ -475,19 +488,21 @@
                 rung_copy(f, s, i).wait_recv()
                 pl.when(has_fwd)(lambda: rail_copy(f, s, i).start())
                 pass_tile(f, s, i)
-            if s + AHEAD < STEPS:
-                send_block(f, s + AHEAD)
-            else:
-                pl.when(f == 0)(lambda: send_block(1, s + AHEAD - STEPS))
-            if s == 3:
-                pl.when(f == 0)(lambda: own_columns(1))
-            if s == 0:
-                pl.when(f == 1)(lambda: finish(0))
-            tasks(f, s)
+                if i == PIECES[s] - 1:
+                    if s + AHEAD < STEPS:
+                        send_block(f, s + AHEAD)
+                    else:
+                        pl.when(f == 0)(lambda: send_block(1, s + AHEAD - STEPS))
+                    if s == 3:
+                        pl.when(f == 0)(lambda: own_columns(1))
+                if (s, i) in late_at:
+                    pl.when(f == 1)(lambda: late(0, late_at[s, i]))
+                early(f, s, i)
         return carry
 
     lax.fori_loop(0, 2, field_steps, 0)
-    finish(1)
+    for part in range(4):
+        late(1, part)
 
     def drain(f, carry):
         for s in range(STEPS):
@@ -527,7 +542,7 @@
         out_specs=pl.BlockSpec(memory_space=pltpu.VMEM),
         scratch_shapes=[
             pltpu.VMEM((2, 6 * T, 8 * T), jnp.float32),
-            pltpu.VMEM((4 * T, 6 * T), jnp.float32),
+            pltpu.VMEM((2, 4 * T, 6 * T), jnp.float32),
             pltpu.VMEM((21, 4 * T, LANES), jnp.float32),
             pltpu.VMEM((16, 6 * T), jnp.float32),
             pltpu.VMEM((LANES, 4 * T), jnp.float32),
@@ -542,7 +557,7 @@
             pltpu.SemaphoreType.DMA((2, sems)),
         ],
         compiler_params=pltpu.CompilerParams(
-            collective_id=0, has_side_effects=True, vmem_limit_bytes=55 * 2**20
+            collective_id=0, has_side_effects=True, vmem_limit_bytes=56 * 2**20
         ),
     )(g_start, cotangent, damping.reshape(1, -1), hopping, bonds, source)
     return pl.pallas_call(

time: 116 us -> 111 us (0.957)
  Pallas kernels: 115 us -> 110 us
    pallas_call x1, Pallas kernels: 113 us -> 108 us  [shards(): pl.pallas_call(functools.partial(kernel, T, n_rows, n_cols, group), out_s...]
where the time goes in v4:
time: 111 us; the launch traced here: 110 us
  Pallas kernels  110 us (99%)
    pallas_call x1, Pallas kernels, shards(): pl.pallas_call(functools.partial(kernel, T, n_rows, n_cols, group), out_s...  108 us

profile of v4, /device:TPU:6, one launch (start us, length us, event | category | flops | bytes accessed | tf_op | source)
XLA Modules:
  0.0 110.4 jit_solution(6031819157320892751)
XLA Ops:
  0.6 107.6 %shard_map.77.fin = f32[2,512,1024]{2,1,0:T(8,128)S(1)} custom-call(f32[512,1024]{1,0:T(8,128)} %g_hbm.1, f32[512,1024]{1,0:T(8,128)} %c_hbm.1, f32[1,32768]{1,0:T(1,128)} %bitcast.1, f32[6,32768]{1,0:T(8,128)} %hopping.1, s32[7,32768]{1,0:T(8,128)} %bonds.1, f32[7,32768]{1,0:T(8,128)} %source.1), custom_call_target="tpu_custom_call" | custom-call | tf_op jit(solution)/shard_map/pallas_call | solution.py:538
  108.2 2.0 %shard_map.78 = (f32[512,1024]{1,0:T(8,128)}, f32[512,1024]{1,0:T(8,128)}) custom-call(f32[2,512,1024]{2,1,0:T(8,128)S(1)} %shard_map.77.fin), custom_call_target="tpu_custom_call" | custom-call | tf_op jit(solution)/shard_map/pallas_call | solution.py:563

commit v5 on v4

--- a/solution.py
+++ b/solution.py
@@ -13,6 +13,7 @@
 STEPS = 8
 AHEAD = 3
 PIECES = (4, 2, 2, 2, 2, 2, 2, 4)
+STORES = 4
 EXTRA = sum(PIECES) - STEPS
 CHUNK = 32
 LANES = 128
@@ -219,7 +220,17 @@
         return jnp.concatenate([band] * (T // LANES), axis=1)
 
     def rate(f, src, row, col, coef_row, col_bands):
-        wide = src[pl.ds(row, CHUNK), pl.ds(aligned(col - LANES, LANES), T + 2 * LANES)]
+        parts = [
+            src[pl.ds(row, CHUNK), pl.ds(aligned(col + (q - 1) * LANES, LANES), LANES)] for q in range(T // LANES + 2)
+        ]
+        lane = lax.broadcasted_iota(jnp.int32, (CHUNK, LANES), 1)
+
+        def shifted(offset):
+            low = 1 if offset > 0 else 0
+            turned = [pltpu.roll(part, (-offset) % LANES, 1) for part in parts[low : low + T // LANES + 1]]
+            keep = lane < (-offset) % LANES
+            return jnp.concatenate([jnp.where(keep, a, b) for a, b in zip(turned[:-1], turned[1:])], axis=1)
+
         tall = src[pl.ds(aligned(row - 8, 8), CHUNK + 16), pl.ds(col, T)]
 
         def rows_of(k):
@@ -231,7 +242,7 @@
                 continue
             if abs(offset) < 8:
                 by_row = pltpu.roll(tall, (-offset) % (CHUNK + 16), 0)[8 : 8 + CHUNK]
-                by_col = pltpu.roll(wide, (-offset) % (T + 2 * LANES), 1)[:, LANES : LANES + T]
+                by_col = shifted(offset)
             else:
                 by_row = src[pl.ds(aligned(row + offset, CHUNK), CHUNK), pl.ds(col, T)]
                 by_col = src[pl.ds(row, CHUNK), pl.ds(aligned(col + offset), T)]
@@ -352,32 +363,36 @@
             wait_tile(f, 1, 0, half_a)
             wait_tile(f, 1, 1, half_b)
             mids(f, ((0, 0), (2, 3), (1, 4)))
-        if s == 6 and last:
+        if s == 6 and i == 0:
             wait_tile(f, 0, 0, half_a)
             wait_tile(f, 0, 1, half_b)
             mids(f, ((1, -1), (2, 0)))
-        if s == 7 and i == 0:
+        if s == 6 and last:
             wait_rail(f, 5)
             mids(f, ((2, 2), (0, 3)))
-        if s == 7 and i == 1:
+            outs(f, ((1, 0),))
+        if s == 7 and i == 0:
             wait_a_corner(f, 1)
             mids(f, ((3, 3),))
+            outs(f, ((1, 3),))
+        if s == 7 and i == 1:
+            wait_a_corner(f, 0)
+            wait_tile(f, 0, 1, half_a)
+            mids(f, ((2, -1),))
         if s == 7 and i == 2:
-            outs(f, ((1, 0), (1, 3)))
+            wait_rail(f, 6)
+            mids(f, ((0, 2),))
+            outs(f, ((1, 2),))
 
     def late(f, part):
         if part == 0:
-            wait_a_corner(f, 0)
             mids(f, ((2, 1), (3, 0), (3, 1), (3, 2)))
         if part == 1:
-            wait_rail(f, 6)
-            mids(f, ((0, 2),))
-            outs(f, ((0, 1), (0, 2), (1, 2)))
+            outs(f, ((0, 0), (0, 1), (0, 2)))
         if part == 2:
-            wait_tile(f, 0, 1, half_a)
             wait_tile(f, 1, 1, half_a)
-            mids(f, ((2, -1), (2, 4)))
-            outs(f, ((0, 0), (0, 3)))
+            mids(f, ((2, 4),))
+            outs(f, ((0, 3),))
         if part == 3:
             wait_rail(f, 7)
             mids(f, ((0, 1),))
@@ -523,7 +538,12 @@
 
 
 def store_kernel(fin, g_out, c_out, sem):
-    copies = [pltpu.make_async_copy(fin.at[k], out, sem.at[k]) for k, out in enumerate((g_out, c_out))]
+    rows = g_out.shape[0] // STORES
+    copies = [
+        pltpu.make_async_copy(fin.at[k, pl.ds(i * rows, rows)], out.at[pl.ds(i * rows, rows)], sem.at[k, i])
+        for i in range(STORES)
+        for k, out in enumerate((g_out, c_out))
+    ]
     for copy in copies:
         copy.start()
     for copy in copies:
@@ -565,7 +585,7 @@
         out_shape=(block, block),
         in_specs=[pl.BlockSpec(memory_space=pltpu.VMEM)],
         out_specs=(anywhere, anywhere),
-        scratch_shapes=[pltpu.SemaphoreType.DMA((2,))],
+        scratch_shapes=[pltpu.SemaphoreType.DMA((2, STORES))],
         compiler_params=pltpu.CompilerParams(vmem_limit_bytes=2**20),
     )(fin)
 

time: 111 us -> 111 us (level)
  no operation moved by 1% of the time
where the time goes in v5:
time: 111 us; the launch traced here: 110 us
  Pallas kernels  110 us (99%)
    pallas_call x1, Pallas kernels, shards(): pl.pallas_call(functools.partial(kernel, T, n_rows, n_cols, group), out_s...  108 us

profile of v5, /device:TPU:6, one launch (start us, length us, event | category | flops | bytes accessed | tf_op | source)
XLA Modules:
  0.0 110.4 jit_solution(343417960935738268)
XLA Ops:
  0.6 107.5 %shard_map.77.fin = f32[2,512,1024]{2,1,0:T(8,128)S(1)} custom-call(f32[512,1024]{1,0:T(8,128)} %g_hbm.1, f32[512,1024]{1,0:T(8,128)} %c_hbm.1, f32[1,32768]{1,0:T(1,128)} %bitcast.1, f32[6,32768]{1,0:T(8,128)} %hopping.1, s32[7,32768]{1,0:T(8,128)} %bonds.1, f32[7,32768]{1,0:T(8,128)} %source.1), custom_call_target="tpu_custom_call" | custom-call | tf_op jit(solution)/shard_map/pallas_call | solution.py:558
  108.1 2.1 %shard_map.78 = (f32[512,1024]{1,0:T(8,128)}, f32[512,1024]{1,0:T(8,128)}) custom-call(f32[2,512,1024]{2,1,0:T(8,128)S(1)} %shard_map.77.fin), custom_call_target="tpu_custom_call" | custom-call | tf_op jit(solution)/shard_map/pallas_call | solution.py:583
